TPU v7x, 256 devices: a whole 4x4x8 slice. The times are simulated.
256 devices in a mesh: ka: 8 (over y_hi, x), band: 32 (over y_lo, z, core).
Axes of the slice: x: 4, y: 4 (y_hi: 2, y_lo: 2; y = y_hi * 2 + y_lo), z: 8, core: 2. Of those that a mesh axis runs over, the one named last changes fastest.
Arguments:
- targets: float32 [256, 2, 24, 576], P(('ka', 'band')), may hold values from -6 to 6
- occupied: bfloat16 [256, 2, 24, 576], P(('ka', 'band')), may hold values from -3 to 3
- kernels: float32 [16, 24, 576], replicated, may hold values from 0.1 to 2
- partner: int32 [8], replicated, may hold values from 0 to 7, as said below
- kernel_index: int32 [16, 16], replicated, may hold values from 0 to 15
Outputs:
- exchange: float32 [256, 2, 24, 576], P(('ka', 'band'))
Inputs may be any that keep to these rules, and one draw needn't show every extreme that they name: partner is a permutation of the groups.
All inputs are finite; a program needn't handle non-finite values.
Results may differ from a plain program's by a relative error of at most 0.0003.
Values may be sent and summed in bfloat16 or wider, within the bound.
A program may use at most 64 MiB of HBM per device.

v0:
```python
import jax
import jax.numpy as jnp
from jax import lax
from jax.sharding import PartitionSpec as P

GRID = 24
KPT_DEV = 2


def passed_along(array, axis, by):
    peers = lax.axis_size(axis)
    return lax.ppermute(array, axis, [(i, (i + by) % peers) for i in range(peers)])


def spectral_tables(grid_size):
    positions = jnp.arange(grid_size, dtype=jnp.int32)
    products = positions[:, None] * positions[None, :] % grid_size
    angles = products.astype(jnp.float32) * (2.0 * jnp.pi / grid_size)
    factor = 1.0 / jnp.sqrt(jnp.float32(grid_size))
    return (jnp.cos(angles) * factor, jnp.sin(angles) * factor)


def rotate_apply(source_field, matrix):
    batch_count, grid_size, plane_size = source_field.shape
    result = lax.dot_general(
        source_field,
        matrix,
        (((1,), (1,)), ((), ())),
        precision=lax.Precision.HIGHEST,
        preferred_element_type=jnp.float32,
    )
    return result.reshape(batch_count, grid_size, plane_size)


def transform(real_part, imag_part, cosine_table, sine_table, direction):
    for repeat in range(3):
        real_part, imag_part = (
            rotate_apply(real_part, cosine_table) - direction * rotate_apply(imag_part, sine_table),
            rotate_apply(imag_part, cosine_table) + direction * rotate_apply(real_part, sine_table),
        )
    return (real_part, imag_part)


def pair_term(orbital, target_real, target_imag, kernel, cosine_table, sine_table):
    orbital_values = orbital.astype(jnp.float32)
    orbital_real = orbital_values[0, 0]
    orbital_imag = orbital_values[0, 1]
    dens_real = orbital_real * target_real + orbital_imag * target_imag
    dens_imag = orbital_real * target_imag - orbital_imag * target_real
    spec_real, spec_imag = transform(dens_real, dens_imag, cosine_table, sine_table, -1.0)
    pot_real, pot_imag = transform(
        kernel * spec_real, kernel * spec_imag, cosine_table, sine_table, 1.0
    )
    return (
        orbital_real * pot_real - orbital_imag * pot_imag,
        orbital_real * pot_imag + orbital_imag * pot_real,
    )


def shards(targets, occupied, kernels, partner, kernel_index):
    band_count = lax.axis_size("band")
    per_kpoint = band_count // KPT_DEV
    my_group = lax.axis_index("ka")
    position = lax.axis_index("band")
    kpoint = my_group * KPT_DEV + position // per_kpoint
    cosine_table, sine_table = spectral_tables(GRID)
    target_real = targets[:, 0]
    target_imag = targets[:, 1]
    everyone = lax.all_gather(occupied, "ka", axis=0, tiled=True)
    partner_group = partner[my_group]
    visitor = lax.dynamic_slice_in_dim(everyone, partner_group, 1, 0)

    def contribute(totals, orbital, source_band):
        source_k = partner_group * KPT_DEV + source_band // per_kpoint
        table_row = kernel_index[kpoint, source_k]
        kernel = lax.dynamic_index_in_dim(kernels, table_row, 0, keepdims=False)
        more_real, more_imag = pair_term(
            orbital, target_real, target_imag, kernel, cosine_table, sine_table
        )
        return (totals[0] - more_real, totals[1] - more_imag)

    empty_field = jnp.zeros_like(target_real)
    totals = contribute((empty_field, empty_field), visitor, position)

    def onward(number, carried):
        current, summed = carried
        current = passed_along(current, "band", 1)
        return (current, contribute(summed, current, (position - number) % band_count))

    current, totals = lax.fori_loop(1, band_count, onward, (visitor, totals))
    return jnp.stack(totals, axis=1)


def solution(mesh):
    return jax.shard_map(
        shards,
        mesh=mesh,
        in_specs=(
            P(("ka", "band"), None, None, None),
            P(("ka", "band"), None, None, None),
            P(),
            P(),
            P(),
        ),
        out_specs=P(("ka", "band"), None, None, None),
        check_vma=False,
    )
```

profile of v0, /device:TPU:1, one launch (start us, length us, event | category | flops | bytes accessed | tf_op | source)
XLA Modules:
  0.0 547.0 jit_solution(14453901876114819552)
XLA Ops:
  6.8 29.9 %all_gather.3 = bf16[8,2,24,576]{3,2,1,0:T(8,128)(2,1)S(1)} all-gather(bf16[1,2,24,576]{3,2,1,0:T(8,128)(2,1)S(1)} %copy-done.2), channel_id=1, replica_groups=mesh['ka'=8,'band'=32] {'ka'}, dimensions={0}, use_global_device_ids=true | all-gather | bytes 497664 | tf_op jit(solution)/shard_map/all_gather | solution.py:69
  47.7 498.6 %while.21 = (s32[]{:T(128)}, bf16[1,2,24,576]{3,2,1,0:T(8,128)(2,1)S(1)}, f32[1,24,576]{2,1,0:T(8,128)S(1)}, f32[1,24,576]{2,1,0:T(8,128)S(1)}, s32[]{:T(128)}, ...) while((s32[]{:T(128)}, ...), condition=%wide.region_1.2_spmd.clone.clone, body=%wide.region_0.1_spmd.clone.clone.sunk | while | flops 96215040 | bytes 7526992 | solution.py:90
  47.9 8.8 %collective-permute-start = (bf16[1,2,24,576]{3,2,1,0:T(8,128)(2,1)S(1)}, bf16[1,2,24,576]{3,2,1,0:T(8,128)(2,1)S(1)}, u32[]{:S(2)}, u32[]{:S(2)}) collective-permute-start(bf16[1,2,24,576]{3,2,1,0:T(8,128)(2,1)S(1)} %get-tuple-element.598), channel_id=1, source_target_pairs={{0,1},{1,2},{2,3},{3,4},{4,5},{5,6},{6,7},{7,8},{8,9},{9,10},{10,1... | collective-permute-start | bytes 165896 | tf_op jit(solution)/shard_map/while/body/eval_jaxpr/ppermute | solution.py:12
  83.9 1.7 collective-permute-start
  102.7 2.2 collective-permute-done
  115.1 1.3 dynamic_slice.80
  118.3 2.5 collective-permute-done
  131.1 1.3 dynamic_slice.80
  134.3 2.5 collective-permute-done
  147.1 1.3 dynamic_slice.80
  150.3 2.5 collective-permute-done
  163.1 1.3 dynamic_slice.80
  166.3 2.5 collective-permute-done
  179.0 1.3 dynamic_slice.80
  182.2 2.5 collective-permute-done
  195.0 1.3 dynamic_slice.80
  198.2 2.5 collective-permute-done
  211.0 1.3 dynamic_slice.80
  214.2 2.5 collective-permute-done
  227.0 1.3 dynamic_slice.80
  230.2 2.5 collective-permute-done
  242.9 1.3 dynamic_slice.80
  246.1 2.5 collective-permute-done
  258.9 1.3 dynamic_slice.80
  262.1 2.5 collective-permute-done
  274.9 1.3 dynamic_slice.80
  278.1 2.5 collective-permute-done
  290.9 1.3 dynamic_slice.80
  294.1 2.5 collective-permute-done
  310.0 2.5 collective-permute-done
  326.0 2.5 collective-permute-done
  342.0 2.5 collective-permute-done
  354.8 1.3 dynamic_slice.80
  358.0 2.5 collective-permute-done
  370.7 1.3 dynamic_slice.80
  373.9 2.5 collective-permute-done
  389.9 2.5 collective-permute-done
  405.9 2.5 collective-permute-done
  421.9 2.5 collective-permute-done
  437.8 2.5 collective-permute-done
  450.6 1.3 dynamic_slice.80
  453.8 2.5 collective-permute-done
  466.6 1.3 dynamic_slice.80
  469.8 2.5 collective-permute-done
  485.8 2.5 collective-permute-done
  501.7 2.5 collective-permute-done
  517.7 2.5 collective-permute-done
  533.7 2.5 collective-permute-done
  (1719 shorter events, 339.3 us)
Async XLA Ops:
  0.0 6.8 %copy-start.2 = (bf16[1,2,24,576]{3,2,1,0:T(8,128)(2,1)S(1)}, bf16[1,2,24,576]{3,2,1,0:T(8,128)(2,1)}, u32[]{:S(2)}) copy-start(bf16[1,2,24,576]{3,2,1,0:T(8,128)(2,1)} %param.8) | copy-start | bytes 165892
  36.7 0.9 copy-start.1
  40.9 1.4 copy-start
  47.9 12.0 %collective-permute-start = (bf16[1,2,24,576]{3,2,1,0:T(8,128)(2,1)S(1)}, bf16[1,2,24,576]{3,2,1,0:T(8,128)(2,1)S(1)}, u32[]{:S(2)}, u32[]{:S(2)}) collective-permute-start(bf16[1,2,24,576]{3,2,1,0:T(8,128)(2,1)S(1)} %get-tuple-element.598), channel_id=1, source_target_pairs={{0,1},{1,2},{2,3},{3,4},{4,5},{5,6},{6,7},{7,8},{8,9},{9,10},{10,1... | collective-permute-start | bytes 165896 | tf_op jit(solution)/shard_map/while/body/eval_jaxpr/ppermute | solution.py:12
  70.1 3.7 collective-permute-start
  83.9 5.0 collective-permute-start
  99.0 5.8 %collective-permute-start = (bf16[1,2,24,576]{3,2,1,0:T(8,128)(2,1)S(1)}, bf16[1,2,24,576]{3,2,1,0:T(8,128)(2,1)S(1)}, u32[]{:S(2)}, u32[]{:S(2)}) collective-permute-start(bf16[1,2,24,576]{3,2,1,0:T(8,128)(2,1)S(1)} %get-tuple-element.598), channel_id=1, source_target_pairs={{0,1},{1,2},{2,3},{3,4},{4,5},{5,6},{6,7},{7,8},{8,9},{9,10},{10,1... | collective-permute-start | bytes 165896 | tf_op jit(solution)/shard_map/while/body/eval_jaxpr/ppermute | solution.py:12
  115.0 5.8 %collective-permute-start = (bf16[1,2,24,576]{3,2,1,0:T(8,128)(2,1)S(1)}, bf16[1,2,24,576]{3,2,1,0:T(8,128)(2,1)S(1)}, u32[]{:S(2)}, u32[]{:S(2)}) collective-permute-start(bf16[1,2,24,576]{3,2,1,0:T(8,128)(2,1)S(1)} %get-tuple-element.598), channel_id=1, source_target_pairs={{0,1},{1,2},{2,3},{3,4},{4,5},{5,6},{6,7},{7,8},{8,9},{9,10},{10,1... | collective-permute-start | bytes 165896 | tf_op jit(solution)/shard_map/while/body/eval_jaxpr/ppermute | solution.py:12
  131.0 5.8 %collective-permute-start = (bf16[1,2,24,576]{3,2,1,0:T(8,128)(2,1)S(1)}, bf16[1,2,24,576]{3,2,1,0:T(8,128)(2,1)S(1)}, u32[]{:S(2)}, u32[]{:S(2)}) collective-permute-start(bf16[1,2,24,576]{3,2,1,0:T(8,128)(2,1)S(1)} %get-tuple-element.598), channel_id=1, source_target_pairs={{0,1},{1,2},{2,3},{3,4},{4,5},{5,6},{6,7},{7,8},{8,9},{9,10},{10,1... | collective-permute-start | bytes 165896 | tf_op jit(solution)/shard_map/while/body/eval_jaxpr/ppermute | solution.py:12
  146.9 5.8 %collective-permute-start = (bf16[1,2,24,576]{3,2,1,0:T(8,128)(2,1)S(1)}, bf16[1,2,24,576]{3,2,1,0:T(8,128)(2,1)S(1)}, u32[]{:S(2)}, u32[]{:S(2)}) collective-permute-start(bf16[1,2,24,576]{3,2,1,0:T(8,128)(2,1)S(1)} %get-tuple-element.598), channel_id=1, source_target_pairs={{0,1},{1,2},{2,3},{3,4},{4,5},{5,6},{6,7},{7,8},{8,9},{9,10},{10,1... | collective-permute-start | bytes 165896 | tf_op jit(solution)/shard_map/while/body/eval_jaxpr/ppermute | solution.py:12
  162.9 5.8 %collective-permute-start = (bf16[1,2,24,576]{3,2,1,0:T(8,128)(2,1)S(1)}, bf16[1,2,24,576]{3,2,1,0:T(8,128)(2,1)S(1)}, u32[]{:S(2)}, u32[]{:S(2)}) collective-permute-start(bf16[1,2,24,576]{3,2,1,0:T(8,128)(2,1)S(1)} %get-tuple-element.598), channel_id=1, source_target_pairs={{0,1},{1,2},{2,3},{3,4},{4,5},{5,6},{6,7},{7,8},{8,9},{9,10},{10,1... | collective-permute-start | bytes 165896 | tf_op jit(solution)/shard_map/while/body/eval_jaxpr/ppermute | solution.py:12
  178.9 5.8 %collective-permute-start = (bf16[1,2,24,576]{3,2,1,0:T(8,128)(2,1)S(1)}, bf16[1,2,24,576]{3,2,1,0:T(8,128)(2,1)S(1)}, u32[]{:S(2)}, u32[]{:S(2)}) collective-permute-start(bf16[1,2,24,576]{3,2,1,0:T(8,128)(2,1)S(1)} %get-tuple-element.598), channel_id=1, source_target_pairs={{0,1},{1,2},{2,3},{3,4},{4,5},{5,6},{6,7},{7,8},{8,9},{9,10},{10,1... | collective-permute-start | bytes 165896 | tf_op jit(solution)/shard_map/while/body/eval_jaxpr/ppermute | solution.py:12
  194.9 5.8 %collective-permute-start = (bf16[1,2,24,576]{3,2,1,0:T(8,128)(2,1)S(1)}, bf16[1,2,24,576]{3,2,1,0:T(8,128)(2,1)S(1)}, u32[]{:S(2)}, u32[]{:S(2)}) collective-permute-start(bf16[1,2,24,576]{3,2,1,0:T(8,128)(2,1)S(1)} %get-tuple-element.598), channel_id=1, source_target_pairs={{0,1},{1,2},{2,3},{3,4},{4,5},{5,6},{6,7},{7,8},{8,9},{9,10},{10,1... | collective-permute-start | bytes 165896 | tf_op jit(solution)/shard_map/while/body/eval_jaxpr/ppermute | solution.py:12
  210.8 5.8 %collective-permute-start = (bf16[1,2,24,576]{3,2,1,0:T(8,128)(2,1)S(1)}, bf16[1,2,24,576]{3,2,1,0:T(8,128)(2,1)S(1)}, u32[]{:S(2)}, u32[]{:S(2)}) collective-permute-start(bf16[1,2,24,576]{3,2,1,0:T(8,128)(2,1)S(1)} %get-tuple-element.598), channel_id=1, source_target_pairs={{0,1},{1,2},{2,3},{3,4},{4,5},{5,6},{6,7},{7,8},{8,9},{9,10},{10,1... | collective-permute-start | bytes 165896 | tf_op jit(solution)/shard_map/while/body/eval_jaxpr/ppermute | solution.py:12
  226.8 5.8 %collective-permute-start = (bf16[1,2,24,576]{3,2,1,0:T(8,128)(2,1)S(1)}, bf16[1,2,24,576]{3,2,1,0:T(8,128)(2,1)S(1)}, u32[]{:S(2)}, u32[]{:S(2)}) collective-permute-start(bf16[1,2,24,576]{3,2,1,0:T(8,128)(2,1)S(1)} %get-tuple-element.598), channel_id=1, source_target_pairs={{0,1},{1,2},{2,3},{3,4},{4,5},{5,6},{6,7},{7,8},{8,9},{9,10},{10,1... | collective-permute-start | bytes 165896 | tf_op jit(solution)/shard_map/while/body/eval_jaxpr/ppermute | solution.py:12
  242.8 5.8 %collective-permute-start = (bf16[1,2,24,576]{3,2,1,0:T(8,128)(2,1)S(1)}, bf16[1,2,24,576]{3,2,1,0:T(8,128)(2,1)S(1)}, u32[]{:S(2)}, u32[]{:S(2)}) collective-permute-start(bf16[1,2,24,576]{3,2,1,0:T(8,128)(2,1)S(1)} %get-tuple-element.598), channel_id=1, source_target_pairs={{0,1},{1,2},{2,3},{3,4},{4,5},{5,6},{6,7},{7,8},{8,9},{9,10},{10,1... | collective-permute-start | bytes 165896 | tf_op jit(solution)/shard_map/while/body/eval_jaxpr/ppermute | solution.py:12
  258.8 5.8 %collective-permute-start = (bf16[1,2,24,576]{3,2,1,0:T(8,128)(2,1)S(1)}, bf16[1,2,24,576]{3,2,1,0:T(8,128)(2,1)S(1)}, u32[]{:S(2)}, u32[]{:S(2)}) collective-permute-start(bf16[1,2,24,576]{3,2,1,0:T(8,128)(2,1)S(1)} %get-tuple-element.598), channel_id=1, source_target_pairs={{0,1},{1,2},{2,3},{3,4},{4,5},{5,6},{6,7},{7,8},{8,9},{9,10},{10,1... | collective-permute-start | bytes 165896 | tf_op jit(solution)/shard_map/while/body/eval_jaxpr/ppermute | solution.py:12
  274.7 5.8 %collective-permute-start = (bf16[1,2,24,576]{3,2,1,0:T(8,128)(2,1)S(1)}, bf16[1,2,24,576]{3,2,1,0:T(8,128)(2,1)S(1)}, u32[]{:S(2)}, u32[]{:S(2)}) collective-permute-start(bf16[1,2,24,576]{3,2,1,0:T(8,128)(2,1)S(1)} %get-tuple-element.598), channel_id=1, source_target_pairs={{0,1},{1,2},{2,3},{3,4},{4,5},{5,6},{6,7},{7,8},{8,9},{9,10},{10,1... | collective-permute-start | bytes 165896 | tf_op jit(solution)/shard_map/while/body/eval_jaxpr/ppermute | solution.py:12
  290.7 5.8 %collective-permute-start = (bf16[1,2,24,576]{3,2,1,0:T(8,128)(2,1)S(1)}, bf16[1,2,24,576]{3,2,1,0:T(8,128)(2,1)S(1)}, u32[]{:S(2)}, u32[]{:S(2)}) collective-permute-start(bf16[1,2,24,576]{3,2,1,0:T(8,128)(2,1)S(1)} %get-tuple-element.598), channel_id=1, source_target_pairs={{0,1},{1,2},{2,3},{3,4},{4,5},{5,6},{6,7},{7,8},{8,9},{9,10},{10,1... | collective-permute-start | bytes 165896 | tf_op jit(solution)/shard_map/while/body/eval_jaxpr/ppermute | solution.py:12
  306.7 5.8 %collective-permute-start = (bf16[1,2,24,576]{3,2,1,0:T(8,128)(2,1)S(1)}, bf16[1,2,24,576]{3,2,1,0:T(8,128)(2,1)S(1)}, u32[]{:S(2)}, u32[]{:S(2)}) collective-permute-start(bf16[1,2,24,576]{3,2,1,0:T(8,128)(2,1)S(1)} %get-tuple-element.598), channel_id=1, source_target_pairs={{0,1},{1,2},{2,3},{3,4},{4,5},{5,6},{6,7},{7,8},{8,9},{9,10},{10,1... | collective-permute-start | bytes 165896 | tf_op jit(solution)/shard_map/while/body/eval_jaxpr/ppermute | solution.py:12
  322.7 5.8 %collective-permute-start = (bf16[1,2,24,576]{3,2,1,0:T(8,128)(2,1)S(1)}, bf16[1,2,24,576]{3,2,1,0:T(8,128)(2,1)S(1)}, u32[]{:S(2)}, u32[]{:S(2)}) collective-permute-start(bf16[1,2,24,576]{3,2,1,0:T(8,128)(2,1)S(1)} %get-tuple-element.598), channel_id=1, source_target_pairs={{0,1},{1,2},{2,3},{3,4},{4,5},{5,6},{6,7},{7,8},{8,9},{9,10},{10,1... | collective-permute-start | bytes 165896 | tf_op jit(solution)/shard_map/while/body/eval_jaxpr/ppermute | solution.py:12
  338.6 5.8 %collective-permute-start = (bf16[1,2,24,576]{3,2,1,0:T(8,128)(2,1)S(1)}, bf16[1,2,24,576]{3,2,1,0:T(8,128)(2,1)S(1)}, u32[]{:S(2)}, u32[]{:S(2)}) collective-permute-start(bf16[1,2,24,576]{3,2,1,0:T(8,128)(2,1)S(1)} %get-tuple-element.598), channel_id=1, source_target_pairs={{0,1},{1,2},{2,3},{3,4},{4,5},{5,6},{6,7},{7,8},{8,9},{9,10},{10,1... | collective-permute-start | bytes 165896 | tf_op jit(solution)/shard_map/while/body/eval_jaxpr/ppermute | solution.py:12
  354.6 5.8 %collective-permute-start = (bf16[1,2,24,576]{3,2,1,0:T(8,128)(2,1)S(1)}, bf16[1,2,24,576]{3,2,1,0:T(8,128)(2,1)S(1)}, u32[]{:S(2)}, u32[]{:S(2)}) collective-permute-start(bf16[1,2,24,576]{3,2,1,0:T(8,128)(2,1)S(1)} %get-tuple-element.598), channel_id=1, source_target_pairs={{0,1},{1,2},{2,3},{3,4},{4,5},{5,6},{6,7},{7,8},{8,9},{9,10},{10,1... | collective-permute-start | bytes 165896 | tf_op jit(solution)/shard_map/while/body/eval_jaxpr/ppermute | solution.py:12
  370.6 5.8 %collective-permute-start = (bf16[1,2,24,576]{3,2,1,0:T(8,128)(2,1)S(1)}, bf16[1,2,24,576]{3,2,1,0:T(8,128)(2,1)S(1)}, u32[]{:S(2)}, u32[]{:S(2)}) collective-permute-start(bf16[1,2,24,576]{3,2,1,0:T(8,128)(2,1)S(1)} %get-tuple-element.598), channel_id=1, source_target_pairs={{0,1},{1,2},{2,3},{3,4},{4,5},{5,6},{6,7},{7,8},{8,9},{9,10},{10,1... | collective-permute-start | bytes 165896 | tf_op jit(solution)/shard_map/while/body/eval_jaxpr/ppermute | solution.py:12
  386.6 5.8 %collective-permute-start = (bf16[1,2,24,576]{3,2,1,0:T(8,128)(2,1)S(1)}, bf16[1,2,24,576]{3,2,1,0:T(8,128)(2,1)S(1)}, u32[]{:S(2)}, u32[]{:S(2)}) collective-permute-start(bf16[1,2,24,576]{3,2,1,0:T(8,128)(2,1)S(1)} %get-tuple-element.598), channel_id=1, source_target_pairs={{0,1},{1,2},{2,3},{3,4},{4,5},{5,6},{6,7},{7,8},{8,9},{9,10},{10,1... | collective-permute-start | bytes 165896 | tf_op jit(solution)/shard_map/while/body/eval_jaxpr/ppermute | solution.py:12
  402.5 5.8 %collective-permute-start = (bf16[1,2,24,576]{3,2,1,0:T(8,128)(2,1)S(1)}, bf16[1,2,24,576]{3,2,1,0:T(8,128)(2,1)S(1)}, u32[]{:S(2)}, u32[]{:S(2)}) collective-permute-start(bf16[1,2,24,576]{3,2,1,0:T(8,128)(2,1)S(1)} %get-tuple-element.598), channel_id=1, source_target_pairs={{0,1},{1,2},{2,3},{3,4},{4,5},{5,6},{6,7},{7,8},{8,9},{9,10},{10,1... | collective-permute-start | bytes 165896 | tf_op jit(solution)/shard_map/while/body/eval_jaxpr/ppermute | solution.py:12
  418.5 5.8 %collective-permute-start = (bf16[1,2,24,576]{3,2,1,0:T(8,128)(2,1)S(1)}, bf16[1,2,24,576]{3,2,1,0:T(8,128)(2,1)S(1)}, u32[]{:S(2)}, u32[]{:S(2)}) collective-permute-start(bf16[1,2,24,576]{3,2,1,0:T(8,128)(2,1)S(1)} %get-tuple-element.598), channel_id=1, source_target_pairs={{0,1},{1,2},{2,3},{3,4},{4,5},{5,6},{6,7},{7,8},{8,9},{9,10},{10,1... | collective-permute-start | bytes 165896 | tf_op jit(solution)/shard_map/while/body/eval_jaxpr/ppermute | solution.py:12
  434.5 5.8 %collective-permute-start = (bf16[1,2,24,576]{3,2,1,0:T(8,128)(2,1)S(1)}, bf16[1,2,24,576]{3,2,1,0:T(8,128)(2,1)S(1)}, u32[]{:S(2)}, u32[]{:S(2)}) collective-permute-start(bf16[1,2,24,576]{3,2,1,0:T(8,128)(2,1)S(1)} %get-tuple-element.598), channel_id=1, source_target_pairs={{0,1},{1,2},{2,3},{3,4},{4,5},{5,6},{6,7},{7,8},{8,9},{9,10},{10,1... | collective-permute-start | bytes 165896 | tf_op jit(solution)/shard_map/while/body/eval_jaxpr/ppermute | solution.py:12
  450.5 5.8 %collective-permute-start = (bf16[1,2,24,576]{3,2,1,0:T(8,128)(2,1)S(1)}, bf16[1,2,24,576]{3,2,1,0:T(8,128)(2,1)S(1)}, u32[]{:S(2)}, u32[]{:S(2)}) collective-permute-start(bf16[1,2,24,576]{3,2,1,0:T(8,128)(2,1)S(1)} %get-tuple-element.598), channel_id=1, source_target_pairs={{0,1},{1,2},{2,3},{3,4},{4,5},{5,6},{6,7},{7,8},{8,9},{9,10},{10,1... | collective-permute-start | bytes 165896 | tf_op jit(solution)/shard_map/while/body/eval_jaxpr/ppermute | solution.py:12
  466.4 5.8 %collective-permute-start = (bf16[1,2,24,576]{3,2,1,0:T(8,128)(2,1)S(1)}, bf16[1,2,24,576]{3,2,1,0:T(8,128)(2,1)S(1)}, u32[]{:S(2)}, u32[]{:S(2)}) collective-permute-start(bf16[1,2,24,576]{3,2,1,0:T(8,128)(2,1)S(1)} %get-tuple-element.598), channel_id=1, source_target_pairs={{0,1},{1,2},{2,3},{3,4},{4,5},{5,6},{6,7},{7,8},{8,9},{9,10},{10,1... | collective-permute-start | bytes 165896 | tf_op jit(solution)/shard_map/while/body/eval_jaxpr/ppermute | solution.py:12
  482.4 5.8 %collective-permute-start = (bf16[1,2,24,576]{3,2,1,0:T(8,128)(2,1)S(1)}, bf16[1,2,24,576]{3,2,1,0:T(8,128)(2,1)S(1)}, u32[]{:S(2)}, u32[]{:S(2)}) collective-permute-start(bf16[1,2,24,576]{3,2,1,0:T(8,128)(2,1)S(1)} %get-tuple-element.598), channel_id=1, source_target_pairs={{0,1},{1,2},{2,3},{3,4},{4,5},{5,6},{6,7},{7,8},{8,9},{9,10},{10,1... | collective-permute-start | bytes 165896 | tf_op jit(solution)/shard_map/while/body/eval_jaxpr/ppermute | solution.py:12
  498.4 5.8 %collective-permute-start = (bf16[1,2,24,576]{3,2,1,0:T(8,128)(2,1)S(1)}, bf16[1,2,24,576]{3,2,1,0:T(8,128)(2,1)S(1)}, u32[]{:S(2)}, u32[]{:S(2)}) collective-permute-start(bf16[1,2,24,576]{3,2,1,0:T(8,128)(2,1)S(1)} %get-tuple-element.598), channel_id=1, source_target_pairs={{0,1},{1,2},{2,3},{3,4},{4,5},{5,6},{6,7},{7,8},{8,9},{9,10},{10,1... | collective-permute-start | bytes 165896 | tf_op jit(solution)/shard_map/while/body/eval_jaxpr/ppermute | solution.py:12
  514.4 5.8 %collective-permute-start = (bf16[1,2,24,576]{3,2,1,0:T(8,128)(2,1)S(1)}, bf16[1,2,24,576]{3,2,1,0:T(8,128)(2,1)S(1)}, u32[]{:S(2)}, u32[]{:S(2)}) collective-permute-start(bf16[1,2,24,576]{3,2,1,0:T(8,128)(2,1)S(1)} %get-tuple-element.598), channel_id=1, source_target_pairs={{0,1},{1,2},{2,3},{3,4},{4,5},{5,6},{6,7},{7,8},{8,9},{9,10},{10,1... | collective-permute-start | bytes 165896 | tf_op jit(solution)/shard_map/while/body/eval_jaxpr/ppermute | solution.py:12
  530.3 5.8 %collective-permute-start = (bf16[1,2,24,576]{3,2,1,0:T(8,128)(2,1)S(1)}, bf16[1,2,24,576]{3,2,1,0:T(8,128)(2,1)S(1)}, u32[]{:S(2)}, u32[]{:S(2)}) collective-permute-start(bf16[1,2,24,576]{3,2,1,0:T(8,128)(2,1)S(1)} %get-tuple-element.598), channel_id=1, source_target_pairs={{0,1},{1,2},{2,3},{3,4},{4,5},{5,6},{6,7},{7,8},{8,9},{9,10},{10,1... | collective-permute-start | bytes 165896 | tf_op jit(solution)/shard_map/while/body/eval_jaxpr/ppermute | solution.py:12
where the time goes:
time: 551 us; the launch traced here: 547 us
  matrix products  200 us (36%)
  local copies, waits for them, and re-layouts  154 us (28%)
  loops' own time  72.3 us (13%)
  waiting for transfers between devices  69.6 us (13%)
  blocking collectives  29.9 us (5%)
  starting transfers between devices  13.6 us (2%)
    dot_general x768, matrix products, rotate_apply(): lax.dot_general(source_field, matrix, (((1,), (1,)), ((), ())), precision...  200 us
    another operation x1, loops' own time, shards(): current, totals = lax.fori_loop(1, band_count, onward, (visitor, totals))  72.3 us
    ppermute x31, waiting for transfers between devices, passed_along(): lax.ppermute(array, axis, [(i, (i + by) % peers) for i in range(peers)])  69.6 us
    add x384, local copies, waits for them, and re-layouts, transform(): rotate_apply(imag_part, cosine_table)  55.1 us
    sub x384, local copies, waits for them, and re-layouts, transform(): rotate_apply(real_part, cosine_table)  55.1 us
    dynamic_slice x32, local copies, waits for them, and re-layouts, contribute(): table_row = kernel_index[kpoint, source_k]  41.6 us
    all_gather x1, blocking collectives, shards(): everyone = lax.all_gather(occupied, 'ka', axis=0, tiled=True)  29.9 us
    ppermute x31, starting transfers between devices, passed_along(): lax.ppermute(array, axis, [(i, (i + by) % peers) for i in range(peers)])  13.6 us
  transfers between devices with their start and end apart: 31, of which 29 were waited for; matrix products, arithmetic and copies ran while one was open for 7% of the time, Pallas kernels for 0%

commit v1 on v0

v1 whole, which is shorter than its diff:
```python
import functools
import numpy as np
import ml_dtypes
import jax
import jax.numpy as jnp
from jax import lax
from jax.experimental import pallas as pl
from jax.experimental.pallas import tpu as pltpu

G = 24
H = 11
BF = jnp.bfloat16
F32 = jnp.float32


def point_order():
    order = np.full((5, 128), -1, np.int64)
    for t, (sb, sc) in enumerate(((1, 1), (1, -1), (-1, 1), (-1, -1))):
        for b in range(1, 12):
            for c in range(1, 12):
                order[t, (b - 1) * H + c - 1] = (sb * b % G) * G + sc * c % G
    edge = [b * G + c for b in range(G) for c in range(G) if b % 12 == 0 or c % 12 == 0]
    order[4, : len(edge)] = edge
    return order


def half_tables():
    order = point_order()
    core, edge = order[0], order[4]
    rows = np.concatenate([core, edge])
    live = rows >= 0
    b, c = rows // G, rows % G
    theta = 2 * np.pi * (np.outer(b, b) % G) / G
    phi = 2 * np.pi * (np.outer(c, c) % G) / G
    both = 2 * np.pi * ((np.outer(b, b) + np.outer(c, c)) % G) / G
    tables = np.stack([
        np.cos(theta) * np.cos(phi),
        np.cos(theta) * np.sin(phi),
        np.sin(theta) * np.cos(phi),
        -np.sin(theta) * np.sin(phi),
    ])
    tables[0, 128:, 128:] = np.cos(both)[128:, 128:]
    tables[1, 128:, 128:] = np.sin(both)[128:, 128:]
    tables[2:, 128:, 128:] = 0.0
    tables = tables * live[None, :, None] * live[None, None, :]
    high = tables.astype(ml_dtypes.bfloat16)
    low = (tables - high.astype(np.float64)).astype(ml_dtypes.bfloat16)
    return np.concatenate([high, low, high], axis=1)


def spread_table():
    order = point_order().reshape(-1)
    table = np.zeros((576, 640), np.float32)
    for lane, point in enumerate(order):
        if point >= 0:
            table[point, lane] = 1.0
    return table


def fft3(x, s3):
    (ar, ai), (br, bi), (cr, ci) = x
    tr, ti = br + cr, bi + ci
    dr, di = (br - cr) * s3, (bi - ci) * s3
    mr, mi = ar - 0.5 * tr, ai - 0.5 * ti
    return [(ar + tr, ai + ti), (mr + di, mi - dr), (mr - di, mi + dr)]


def add(x, y):
    return (x[0] + y[0], x[1] + y[1])


def sub(x, y):
    return (x[0] - y[0], x[1] - y[1])


def minus_i(x):
    return (x[1], -x[0])


def fft4(x):
    e0, e1 = add(x[0], x[2]), sub(x[0], x[2])
    o0, o1 = add(x[1], x[3]), sub(x[1], x[3])
    return [add(e0, o0), (e1[0] + o1[1], e1[1] - o1[0]), sub(e0, o0), (e1[0] - o1[1], e1[1] + o1[0])]


def fft8(x):
    r = float(np.sqrt(0.5))
    e = fft4([x[0], x[2], x[4], x[6]])
    o = fft4([x[1], x[3], x[5], x[7]])
    o1 = ((o[1][0] + o[1][1]) * r, (o[1][1] - o[1][0]) * r)
    o3 = ((o[3][1] - o[3][0]) * r, (o[3][0] + o[3][1]) * r)
    out = [None] * 8
    out[0], out[4] = add(e[0], o[0]), sub(e[0], o[0])
    out[1], out[5] = add(e[1], o1), sub(e[1], o1)
    out[2], out[6] = (e[2][0] + o[2][1], e[2][1] - o[2][0]), (e[2][0] - o[2][1], e[2][1] + o[2][0])
    out[3], out[7] = (e[3][0] + o3[0], e[3][1] - o3[1]), (e[3][0] - o3[0], e[3][1] + o3[1])
    return out


def fft24(load, store):
    s3 = float(np.sqrt(0.75))
    cols = []
    for n2 in range(8):
        cols.append(fft3([load((8 * n1 + 3 * n2) % 24) for n1 in range(3)], s3))
    for k1 in range(3):
        outs = fft8([cols[n2][k1] for n2 in range(8)])
        for k2 in range(8):
            k = next(k for k in range(24) if k % 3 == k1 and k % 8 == k2)
            store(k, outs[k2])


def split(x):
    high = x.astype(BF)
    return high, (x - high.astype(F32)).astype(BF)


R = 192


def product(xh, xl, w_ref, yc, ye):
    @pl.loop(0, 4)
    def _(p):
        left = jnp.concatenate([xh[p], xh[4], xh[p], xh[4], xl[p], xl[4]], axis=1)
        y = jnp.dot(left, w_ref[p], preferred_element_type=F32)
        yc[p] = y[:, :128]
        ye[p] = y[:, 128:]


def rows(a, n=8):
    return pl.ds(pl.multiple_of(a * 8, 8), n)


def irows(a, n=8):
    return pl.ds(pl.multiple_of(R + a * 8, 8), n)


def batch(base, kq, phi, psi, kern, w_ref, acc, xh, xl, yc, ye, z):
    def orbital(c, t, a):
        return phi[c, t, pl.ds(base * 24 + a, 8, stride=24), :]

    def spread(ref, *where):
        *lead, a = where
        return jnp.broadcast_to(ref[tuple(lead) + (pl.ds(a, 1),)], (8, 128))

    def density(t, a):
        pr, pi = orbital(0, t, a), orbital(1, t, a)
        tr, ti = spread(psi, 0, t, a), spread(psi, 1, t, a)
        return pr * tr + pi * ti, pr * ti - pi * tr

    @pl.loop(0, 12)
    def _(h):
        grid = []
        for t in range(5):
            lo = density(t, 2 * h)
            hi = density(t, 2 * h + 1)
            grid.append([jnp.concatenate([lo[c], hi[c]], axis=0) for c in range(2)])
        for c in range(2):
            pp, pm, mp, mm, edge = (grid[t][c] for t in range(5))
            s, d, u, v = pp + mm, pp - mm, pm + mp, pm - mp
            at = pl.ds(pl.multiple_of(c * R + h * 16, 16), 16)
            for p, x in enumerate((s + u, d - v, d + v, s - u, edge)):
                xh[p, at, :], xl[p, at, :] = split(x)

    product(xh, xl, w_ref, yc, ye)

    def edge_sum(a):
        er = ye[0, rows(a), :] + ye[3, rows(a), :]
        ei = ye[0, irows(a), :] + ye[3, irows(a), :]
        xr = ye[1, rows(a), :] + ye[2, rows(a), :]
        xi = ye[1, irows(a), :] + ye[2, irows(a), :]
        return er, ei, xr, xi

    def forward_edge(a):
        er, ei, xr, xi = edge_sum(a)
        return er + xi, ei - xr

    def keep(p):
        def store(k, x):
            z[p, rows(k), :] = x[0]
            z[p, irows(k), :] = x[1]
        return store

    @pl.loop(0, 4)
    def _(p):
        fft24(lambda a: (yc[p, rows(a), :], yc[p, irows(a), :]), keep(p))

    fft24(forward_edge, keep(4))

    @pl.loop(0, 24)
    def _(a):
        re = [z[p, rows(a), :] for p in range(5)]
        im = [z[p, irows(a), :] for p in range(5)]
        k = [spread(kern, kq, t, a) for t in range(5)]
        pr, qr = re[0] + re[3], re[0] - re[3]
        pi, qi = im[0] + im[3], im[0] - im[3]
        sr, dr = re[2] + re[1], re[2] - re[1]
        si, di = im[2] + im[1], im[2] - im[1]
        for out, (pp, mm, pm, mp) in enumerate((
            (pr + si, pr - si, qr + di, qr - di),
            (pi - sr, pi + sr, qi - dr, qi + dr),
        )):
            pp, pm, mp, mm = pp * k[0], pm * k[1], mp * k[2], mm * k[3]
            s, d, u, v = pp + mm, pp - mm, pm + mp, pm - mp
            at = irows(a) if out else rows(a)
            for p, x in enumerate((s + u, d - v, d + v, s - u)):
                z[p, at, :] = x
        z[4, rows(a), :] = re[4] * k[4]
        z[4, irows(a), :] = im[4] * k[4]

    @pl.loop(0, 5)
    def _(p):
        got = {}

        def store(k, x):
            got[k] = x

        fft24(lambda a: (z[p, irows(a), :], z[p, rows(a), :]), store)
        for h in range(12):
            for c in range(2):
                x = jnp.concatenate([got[2 * h][1 - c], got[2 * h + 1][1 - c]], axis=0)
                at = pl.ds(c * R + h * 16, 16)
                xh[p, at, :], xl[p, at, :] = split(x)

    product(xh, xl, w_ref, yc, ye)

    @pl.loop(0, 24)
    def _(a):
        re = [yc[p, rows(a), :] for p in range(4)]
        im = [yc[p, irows(a), :] for p in range(4)]
        pr, qr = re[0] + re[3], re[0] - re[3]
        pi, qi = im[0] + im[3], im[0] - im[3]
        sr, dr = re[2] + re[1], re[2] - re[1]
        si, di = im[2] + im[1], im[2] - im[1]
        er, ei, xr, xi = edge_sum(a)
        vr = (pr - si, qr - di, qr + di, pr + si, er - xi)
        vi = (pi + sr, qi + dr, qi - dr, pi - sr, ei + xr)
        for t in range(5):
            fr, fi = orbital(0, t, a), orbital(1, t, a)
            acc[t, rows(a), :] += fr * vr[t] - fi * vi[t]
            acc[t, irows(a), :] += fr * vi[t] + fi * vr[t]


SCRATCH = [
    pltpu.VMEM((5, 2 * R, 128), F32),
    pltpu.VMEM((5, 2 * R, 128), BF),
    pltpu.VMEM((5, 2 * R, 128), BF),
    pltpu.VMEM((4, 2 * R, 128), F32),
    pltpu.VMEM((4, 2 * R, 128), F32),
    pltpu.VMEM((5, 2 * R, 128), F32),
    pltpu.VMEM((2, 5, 768, 128), F32),
]


def local_kernel(occ_ref, psi_ref, kern_ref, w_ref, out_ref, acc, xh, xl, yc, ye, z, phi):
    acc[...] = jnp.zeros_like(acc)

    @pl.loop(0, 32)
    def _(i):
        for c in range(2):
            for t in range(5):
                phi[c, t, pl.ds(pl.multiple_of(i * 24, 8), 24), :] = occ_ref[i, c, :, t * 128:(t + 1) * 128].astype(F32)

    @pl.loop(0, 4)
    def _(n):
        batch(n * 8, n // 2, phi, psi_ref, kern_ref, w_ref, acc, xh, xl, yc, ye, z)

    for c in range(2):
        for t in range(5):
            x = acc[t, c * R:(c + 1) * R, :].reshape(24, 8, 128)
            out_ref[c, t] = jnp.sum(x, axis=1)


def compute(occ, psi, kern, w):
    return pl.pallas_call(
        local_kernel,
        out_shape=jax.ShapeDtypeStruct((2, 5, 24, 128), F32),
        in_specs=[pl.BlockSpec(memory_space=pltpu.VMEM)] * 4,
        out_specs=pl.BlockSpec(memory_space=pltpu.VMEM),
        scratch_shapes=SCRATCH,
        compiler_params=pltpu.CompilerParams(vmem_limit_bytes=60 * 2**20),
    )(occ, psi, kern, w)


KPT_DEV = 2


def spread_lanes(x, table):
    y = jnp.dot(x.reshape(-1, 576), table, precision=lax.Precision.HIGHEST, preferred_element_type=F32)
    return y.reshape(x.shape[:-1] + (5, 128))


def shards(targets, occupied, kernels, partner, kernel_index):
    per_kpoint = lax.axis_size("band") // KPT_DEV
    my_group = lax.axis_index("ka")
    kpoint = my_group * KPT_DEV + lax.axis_index("band") // per_kpoint
    table = jnp.asarray(spread_table())
    tables = jnp.asarray(half_tables())
    mine = jnp.dot(
        occupied.reshape(48, 576), table.astype(BF), preferred_element_type=F32
    ).astype(BF).reshape(1, 2, 24, 640)
    everyone = lax.all_gather(mine, "ka", axis=0, tiled=True)
    partner_group = partner[my_group]
    visitor = lax.dynamic_slice_in_dim(everyone, partner_group, 1, 0)
    occ = lax.all_gather(visitor, "band", axis=0, tiled=True)
    psi = spread_lanes(targets[0], table).transpose(0, 2, 1, 3)
    pair = lax.dynamic_slice(kernel_index, (kpoint, partner_group * KPT_DEV), (1, KPT_DEV))[0]
    kern = spread_lanes(kernels[pair] * (-1.0 / 13824.0), table).transpose(0, 2, 1, 3)
    out = compute(occ, psi, kern, tables)
    out = out.transpose(0, 2, 1, 3).reshape(48, 640)
    out = jnp.dot(out, table.T, precision=lax.Precision.HIGHEST, preferred_element_type=F32)
    return out.reshape(1, 2, 24, 576)


def solution(mesh):
    from jax.sharding import PartitionSpec as P
    return jax.shard_map(
        shards,
        mesh=mesh,
        in_specs=(P(("ka", "band"), None, None, None), P(("ka", "band"), None, None, None), P(), P(), P()),
        out_specs=P(("ka", "band"), None, None, None),
        check_vma=False,
    )
```

time: 551 us -> 147 us (0.27)
  matrix products: 200 us -> 7.63 us
  local copies, waits for them, and re-layouts: 154 us -> 2.6 us
  loops' own time: 72.3 us -> 0 us
  Pallas kernels: 0 us -> 21.9 us
  starting transfers between devices: 13.6 us -> 0.01 us
  between operations: 4.63 us -> 16.1 us
    dot_general x768 -> x4, matrix products: 200 us -> 7.63 us  [the longest x2 3.23 us: spread_lanes(): jnp.dot(x.reshape(-1, 576), table, precision=lax.Precision.HIGHEST, prefe...]
    another operation x1 -> x0, loops' own time: 72.3 us -> none  [shards(): current, totals = lax.fori_loop(1, band_count, onward, (visitor, totals))]
    ppermute x31 -> x0, waiting for transfers between devices: 69.6 us -> none  [passed_along(): lax.ppermute(array, axis, [(i, (i + by) % peers) for i in range(peers)])]
    all_gather x0 -> x1, waiting for transfers between devices: none -> 68.1 us  [shards(): occ = lax.all_gather(visitor, 'band', axis=0, tiled=True)]
    add x384 -> x0, local copies, waits for them, and re-layouts: 55.1 us -> none  [transform(): rotate_apply(imag_part, cosine_table)]
    sub x384 -> x0, local copies, waits for them, and re-layouts: 55.1 us -> none  [transform(): rotate_apply(real_part, cosine_table)]
    dynamic_slice x32 -> x1, local copies, waits for them, and re-layouts: 41.6 us -> 0.64 us  [shards(): visitor = lax.dynamic_slice_in_dim(everyone, partner_group, 1, 0)]
    pallas_call x0 -> x1, Pallas kernels: none -> 21.9 us  [compute(): pl.pallas_call(local_kernel, out_shape=jax.ShapeDtypeStruct((2, 5, 24, 12...]
  transfers between devices with their start and end apart: 31 -> 1, of which waited for: 29 -> 1; matrix products, arithmetic and copies ran while one was open for 7% -> 3% of each run, Pallas kernels for 0% -> 0%
where the time goes in v1:
time: 147 us
  waiting for transfers between devices  68.1 us (46%)
  blocking collectives  30 us (20%)
  Pallas kernels  21.9 us (15%)
  between operations  16.1 us (11%)
  matrix products  7.63 us (5%)
  local copies, waits for them, and re-layouts  2.6 us (2%)
    all_gather x1, waiting for transfers between devices, shards(): occ = lax.all_gather(visitor, 'band', axis=0, tiled=True)  68.1 us
    all_gather x1, blocking collectives, shards(): everyone = lax.all_gather(mine, 'ka', axis=0, tiled=True)  30 us
    pallas_call x1, Pallas kernels, compute(): pl.pallas_call(local_kernel, out_shape=jax.ShapeDtypeStruct((2, 5, 24, 12...  21.9 us
    dot_general x2, matrix products, spread_lanes(): jnp.dot(x.reshape(-1, 576), table, precision=lax.Precision.HIGHEST, prefe...  3.23 us
    dot_general x1, matrix products, shards(): jnp.dot(out, table.T, precision=lax.Precision.HIGHEST, preferred_element_...  3 us
  transfers between devices with their start and end apart: 1, of which 1 were waited for; matrix products, arithmetic and copies ran while one was open for 3% of the time, Pallas kernels for 0%

profile of v1, /device:TPU:1, one launch (start us, length us, event | category | flops | bytes accessed | tf_op | source)
XLA Modules:
  0.0 147.1 jit_solution(10330251262064922538)
XLA Ops:
  6.5 0.0 copy-start
  6.5 0.0 copy-start.1
  6.5 0.0 all-gather.2.cloned.1.call-start
  6.5 1.4 dynamic_slice.9
  9.2 1.4 convolution_convert_fusion
  10.6 0.0 copy-start.3
  10.6 30.0 %all_gather.6 = bf16[8,2,24,640]{3,2,1,0:T(8,128)(2,1)S(1)} all-gather(bf16[1,2,24,640]{3,2,1,0:T(8,128)(2,1)S(1)} %bitcast.41), channel_id=1, replica_groups=mesh['ka'=8,'band'=32] {'ka'}, dimensions={0}, use_global_device_ids=true | all-gather | bytes 552960 | tf_op jit(solution)/shard_map/all_gather | solution.py:301
  41.3 0.6 constant_dynamic-slice_fusion
  42.0 0.0 all-gather.2.cloned.1.call-update
  42.7 0.8 fusion.2
  43.5 0.0 copy-done
  43.5 0.6 gather_fusion
  44.0 0.0 copy-done.1
  44.0 1.6 %convolution_bitcast_fusion.1.kern_ref = f32[2,5,24,128]{3,2,1,0:T(8,128)} fusion(f32[5,128,576,1]{1,2,0,3:T(8,128)S(1)} %copy-done.1, f32[2,24,576]{2,1,0:T(8,128)S(1)} %gather_fusion), kind=kOutput, calls=%fused_computation.2 | convolution fusion | flops 212364288 | bytes 1708032 | tf_op jit(solution)/shard_map/dot_general | solution.py:288
  45.6 0.0 copy-done.3
  45.6 1.7 %convolution_bitcast_fusion.2.psi_ref = f32[2,5,24,128]{3,2,1,0:T(8,128)} fusion(f32[5,128,576,1]{1,2,0,3:T(8,128)S(1)} %copy-done.1, f32[1,2,24,576]{3,2,1,0:T(8,128)S(1)} %copy-done.3), kind=kOutput, calls=%fused_computation.3 | convolution fusion | flops 212336640 | bytes 1708032 | tf_op jit(solution)/shard_map/dot_general | solution.py:288
  47.3 0.0 copy-start.2
  47.3 68.1 %all-gather.2.cloned.1.call-done.occ_ref = bf16[32,2,24,640]{3,2,1,0:T(8,128)(2,1)} async-done(((bf16[1,2,24,640]{3,2,1,0:T(8,128)(2,1)}), bf16[32,2,24,640]{3,2,1,0:T(8,128)(2,1)}) %all-gather.2.cloned.1.call-update) | async-done | bytes 1966096 | tf_op jit(solution)/shard_map/all_gather | solution.py:304
  115.3 21.9 %shard_map.73 = f32[2,5,24,128]{3,2,1,0:T(8,128)} custom-call(bf16[32,2,24,640]{3,2,1,0:T(8,128)(2,1)} %all-gather.2.cloned.1.call-done.occ_ref, f32[2,5,24,128]{3,2,1,0:T(8,128)} %convolution_bitcast_fusion.2.psi_ref, f32[2,5,24,128]{3,2,1,0:T(8,128)} %convolution_bitcast_fusion.1.kern_ref, bf16[4,768,256]{2,1,0:T(8,128)(2,1)} %constant.40.clone.w_ref), custom_call_target="tpu_custom_call" | custom-call | tf_op jit(solution)/shard_map/pallas_call | solution.py:274
  137.3 0.0 copy-done.2
  137.3 3.0 %convolution_bitcast_fusion = f32[1,2,24,576]{3,2,1,0:T(8,128)} fusion(f32[576,640,1]{1,0,2:T(8,128)S(1)} %copy-done.2, f32[2,5,24,128]{3,2,1,0:T(8,128)} %shard_map.73), kind=kOutput, calls=%fused_computation.1 | convolution fusion | flops 212336640 | bytes 1708032 | tf_op jit(solution)/shard_map/dot_general | solution.py:310
  (1 shorter events, 0.0 us)
Async XLA Ops:
  6.5 36.9 %copy-start = (f32[16,24,576]{2,1,0:T(8,128)S(1)}, f32[16,24,576]{2,1,0:T(8,128)}, u32[]{:S(2)}) copy-start(f32[16,24,576]{2,1,0:T(8,128)} %param.9) | copy-start | bytes 2654212
  6.5 37.5 %copy-start.1 = (f32[5,128,576,1]{1,2,0,3:T(8,128)S(1)}, f32[5,128,576,1]{1,2,0,3:T(8,128)}, u32[]{:S(2)}) copy-start(f32[5,128,576,1]{1,2,0,3:T(8,128)} %constant.46) | copy-start | bytes 4423684
  6.5 108.8 %all-gather.2.cloned.1.call-start = ((), (), s32[]{:S(2)}) async-start(), calls=%async_computation | async-start | bytes 2027520 | tf_op jit(solution)/shard_map/all_gather | solution.py:304
  10.6 35.0 %copy-start.3 = (f32[1,2,24,576]{3,2,1,0:T(8,128)S(1)}, f32[1,2,24,576]{3,2,1,0:T(8,128)}, u32[]{:S(2)}) copy-start(f32[1,2,24,576]{3,2,1,0:T(8,128)} %param.7) | copy-start | bytes 331780
  47.3 90.0 %copy-start.2 = (f32[576,640,1]{1,0,2:T(8,128)S(1)}, f32[576,640,1]{1,0,2:T(8,128)}, u32[]{:S(2)}) copy-start(f32[576,640,1]{1,0,2:T(8,128)} %constant.47) | copy-start | bytes 4423684
Sparse Core Ops, SparseCore 0:
  42.1 73.1 all-gather.1

commit v2 on v1

--- a/solution.py
+++ b/solution.py
@@ -45,7 +45,7 @@
     tables = tables * live[None, :, None] * live[None, None, :]
     high = tables.astype(ml_dtypes.bfloat16)
     low = (tables - high.astype(np.float64)).astype(ml_dtypes.bfloat16)
-    return np.concatenate([high, low, high], axis=1)
+    return np.concatenate([high, low], axis=1)
 
 
 def spread_table():
@@ -121,7 +121,8 @@
     @pl.loop(0, 4)
     def _(p):
         left = jnp.concatenate([xh[p], xh[4], xh[p], xh[4], xl[p], xl[4]], axis=1)
-        y = jnp.dot(left, w_ref[p], preferred_element_type=F32)
+        right = jnp.concatenate([w_ref[p], w_ref[p, :256]], axis=0)
+        y = jnp.dot(left, right, preferred_element_type=F32)
         yc[p] = y[:, :128]
         ye[p] = y[:, 128:]
 
@@ -134,17 +135,24 @@
     return pl.ds(pl.multiple_of(R + a * 8, 8), n)
 
 
-def batch(base, kq, phi, psi, kern, w_ref, acc, xh, xl, yc, ye, z):
+def batch(n, hook, blocks, phi, psi, kern, w_ref, acc, xh, xl, yc, ye, z):
+
+    @pl.loop(0, 8)
+    def _(j):
+        for r in range(3):
+            for t in range(5):
+                at = pl.ds(pl.multiple_of(j * 48 + r * 16, 16), 16)
+                phi[t, at, :] = blocks[n * 8 + j, r * 5 + t].astype(F32)
+
     def orbital(c, t, a):
-        return phi[c, t, pl.ds(base * 24 + a, 8, stride=24), :]
-
-    def spread(ref, *where):
-        *lead, a = where
-        return jnp.broadcast_to(ref[tuple(lead) + (pl.ds(a, 1),)], (8, 128))
+        return phi[t, pl.ds(c * 24 + a, 8, stride=48), :]
+
+    def row(x):
+        return jnp.broadcast_to(x, (8, 128))
 
     def density(t, a):
         pr, pi = orbital(0, t, a), orbital(1, t, a)
-        tr, ti = spread(psi, 0, t, a), spread(psi, 1, t, a)
+        tr, ti = row(psi[t, pl.ds(a, 1), :]), row(psi[t, pl.ds(24 + a, 1), :])
         return pr * tr + pi * ti, pr * ti - pi * tr
 
     @pl.loop(0, 12)
@@ -162,6 +170,7 @@
                 xh[p, at, :], xl[p, at, :] = split(x)
 
     product(xh, xl, w_ref, yc, ye)
+    hook(0)
 
     def edge_sum(a):
         er = ye[0, rows(a), :] + ye[3, rows(a), :]
@@ -186,11 +195,14 @@
 
     fft24(forward_edge, keep(4))
 
+    near = jnp.where(n < 2, 6, jnp.where(n == 2, 4, 0))
+    same = lax.broadcasted_iota(jnp.int32, (8, 128), 0) < near
+
     @pl.loop(0, 24)
     def _(a):
         re = [z[p, rows(a), :] for p in range(5)]
         im = [z[p, irows(a), :] for p in range(5)]
-        k = [spread(kern, kq, t, a) for t in range(5)]
+        k = [jnp.where(same, row(kern[t, pl.ds(a, 1), :]), row(kern[t, pl.ds(24 + a, 1), :])) for t in range(5)]
         pr, qr = re[0] + re[3], re[0] - re[3]
         pi, qi = im[0] + im[3], im[0] - im[3]
         sr, dr = re[2] + re[1], re[2] - re[1]
@@ -222,6 +234,7 @@
                 xh[p, at, :], xl[p, at, :] = split(x)
 
     product(xh, xl, w_ref, yc, ye)
+    hook(1)
 
     @pl.loop(0, 24)
     def _(a):
@@ -239,75 +252,223 @@
             acc[t, rows(a), :] += fr * vr[t] - fi * vi[t]
             acc[t, irows(a), :] += fr * vi[t] + fi * vr[t]
 
-
-SCRATCH = [
-    pltpu.VMEM((5, 2 * R, 128), F32),
-    pltpu.VMEM((5, 2 * R, 128), BF),
-    pltpu.VMEM((5, 2 * R, 128), BF),
-    pltpu.VMEM((4, 2 * R, 128), F32),
-    pltpu.VMEM((4, 2 * R, 128), F32),
-    pltpu.VMEM((5, 2 * R, 128), F32),
-    pltpu.VMEM((2, 5, 768, 128), F32),
+    hook(2)
+
+
+NEAR = [0, 1, -1, 2, -2, 3, -3, 4]
+CHIPS = [
+    (0, 0), (0, 1), (0, -1), (1, 0),
+    (0, 2), (0, -2), (0, 3), (1, 1),
+    (0, -3), (0, 4), (1, -1), (1, 2),
+    (1, -2), (1, 3), (1, -3), (1, 4),
 ]
-
-
-def local_kernel(occ_ref, psi_ref, kern_ref, w_ref, out_ref, acc, xh, xl, yc, ye, z, phi):
+MESH = pl.DeviceIdType.MESH
+
+
+def slot(y, d, c):
+    return CHIPS.index((y, d)) * 2 + c
+
+
+def three_parts(x):
+    high = x.astype(BF)
+    rest = x - high.astype(F32)
+    mid = rest.astype(BF)
+    return high, mid, (rest - mid.astype(F32)).astype(BF)
+
+
+def permute_exact(x, table, dims):
+    total = None
+    for part in three_parts(x):
+        y = lax.dot_general(part, table, (dims, ((), ())), preferred_element_type=F32)
+        total = y if total is None else total + y
+    return total
+
+
+def whole_kernel(partner_ref, index_ref, occ_ref, tgt_ref, kernels_hbm, table_hbm, w_hbm, out_ref,
+                 acc, xh, xl, yc, ye, z, phi, psi, kern, w_ref, table, kernels,
+                 mine, spread, stage, blocks,
+                 load_sem, one_send, one_recv, two_send, two_recv, band_send, band_recv):
+    me = lax.axis_index("ka")
+    band = lax.axis_index("band")
+    core = lax.rem(band, 2)
+    zed = lax.rem(band // 2, 8)
+    why = band // 16
+
+    def at(y, zz, c):
+        return (me, y * 16 + zz * 2 + c)
+
+    below = at(why, lax.rem(zed + 7, 8), core)
+    above = at(why, lax.rem(zed + 1, 8), core)
+    across = at(1 - why, zed, core)
+    sibling = at(why, zed, 1 - core)
+
+    loads = [
+        pltpu.make_async_copy(table_hbm, table, load_sem.at[0]),
+        pltpu.make_async_copy(w_hbm, w_ref, load_sem.at[1]),
+        pltpu.make_async_copy(kernels_hbm, kernels, load_sem.at[2]),
+    ]
+    for load in loads:
+        load.start()
+
+    barrier = pltpu.get_barrier_semaphore()
+    for k in range(1, 8):
+        pl.semaphore_signal(barrier, inc=1, device_id=(lax.rem(me + k, 8), band), device_id_type=MESH)
+    for peer in (below, above, across, sibling):
+        pl.semaphore_signal(barrier, inc=1, device_id=peer, device_id_type=MESH)
+
+    loads[0].wait()
+    own = jnp.dot(occ_ref[...], table[...], preferred_element_type=F32).astype(BF)
+    for r in range(3):
+        for t in range(5):
+            mine[r * 5 + t] = own[r * 16:(r + 1) * 16, t * 128:(t + 1) * 128]
+    mine[15] = jnp.zeros((16, 128), BF)
+    spread[me] = mine[pl.ds(me * 2, 2)]
+
+    pl.semaphore_wait(barrier, 11)
+
+    def piece(src, dst, send, recv, k):
+        return pltpu.make_async_remote_copy(
+            src_ref=src, dst_ref=dst, send_sem=send.at[k], recv_sem=recv.at[k],
+            device_id=(lax.rem(me + k, 8), band), device_id_type=MESH)
+
+    first = [piece(mine.at[pl.ds(lax.rem(me + k, 8) * 2, 2)], spread.at[me], one_send, one_recv, k) for k in range(1, 8)]
+    for copy in first:
+        copy.start()
+
     acc[...] = jnp.zeros_like(acc)
-
-    @pl.loop(0, 32)
-    def _(i):
-        for c in range(2):
-            for t in range(5):
-                phi[c, t, pl.ds(pl.multiple_of(i * 24, 8), 24), :] = occ_ref[i, c, :, t * 128:(t + 1) * 128].astype(F32)
+    psi_all = permute_exact(tgt_ref[...], table[...], ((1,), (0,)))
+    for t in range(5):
+        psi[t] = psi_all[:, t * 128:(t + 1) * 128]
+
+    for copy in first:
+        copy.wait_recv()
+    for g in range(8):
+        stage[g] = spread[partner_ref[g]]
+    blocks[0, pl.ds(me * 2, 2)] = spread[partner_ref[me]]
+    second = [piece(stage.at[lax.rem(me + k, 8)], blocks.at[0, pl.ds(me * 2, 2)], two_send, two_recv, k) for k in range(1, 8)]
+    for copy in second:
+        copy.start()
+
+    loads[2].wait()
+    group = partner_ref[me]
+    kpoint = me * 2 + why
+    scaled = jnp.concatenate(
+        [kernels[index_ref[kpoint, group * 2 + q]] for q in (why, 1 - why)], axis=0) * (-1.0 / 13824.0)
+    kern_all = permute_exact(scaled, table[...], ((1,), (0,)))
+    for t in range(5):
+        kern[t] = kern_all[:, t * 128:(t + 1) * 128]
+    loads[1].wait()
+
+    sent = []
+
+    def send(source, target, peer):
+        copy = pltpu.make_async_remote_copy(
+            src_ref=blocks.at[source, pl.ds(0, 15)], dst_ref=blocks.at[target, pl.ds(0, 15)],
+            send_sem=band_send.at[target], recv_sem=band_recv.at[target],
+            device_id=peer, device_id_type=MESH)
+        copy.start()
+        sent.append(target)
+
+    def arrived(target):
+        pltpu.make_async_remote_copy(
+            src_ref=blocks.at[0, pl.ds(0, 15)], dst_ref=blocks.at[target, pl.ds(0, 15)],
+            send_sem=band_send.at[target], recv_sem=band_recv.at[target],
+            device_id=sibling, device_id_type=MESH).wait_recv()
+
+    def pass_on(y, d):
+        have = slot(y, d, 0)
+        if y == 0:
+            if 0 <= d <= 3:
+                send(have, slot(0, d + 1, 0), below)
+            if -2 <= d <= 0:
+                send(have, slot(0, d - 1, 0), above)
+            send(have, slot(1, d, 0), across)
+        send(have, slot(y, d, 1), sibling)
+
+    def take(*chips):
+        for y, d in chips:
+            arrived(slot(y, d, 0))
+            pass_on(y, d)
+
+    def need(*chips):
+        for y, d in chips:
+            arrived(slot(y, d, 1))
+
+    for copy in second:
+        copy.wait_recv()
+    pass_on(0, 0)
+    take((0, 1), (0, -1), (1, 0))
+    need((0, 0), (0, 1), (0, -1), (1, 0))
+
+    steps = {
+        (0, 0): lambda: take((0, 2), (0, -2), (1, 1), (1, -1)),
+        (0, 1): lambda: take((0, 3), (0, -3), (1, 2), (1, -2)),
+        (0, 2): lambda: need((0, 2), (0, -2), (0, 3), (1, 1)),
+        (1, 0): lambda: take((0, 4), (1, 3), (1, -3)),
+        (1, 1): lambda: take((1, 4)),
+        (1, 2): lambda: need((0, -3), (0, 4), (1, -1), (1, 2)),
+        (2, 2): lambda: need((1, -2), (1, 3), (1, -3), (1, 4)),
+    }
 
     @pl.loop(0, 4)
     def _(n):
-        batch(n * 8, n // 2, phi, psi_ref, kern_ref, w_ref, acc, xh, xl, yc, ye, z)
-
+        def hook(place):
+            for (when, where), step in steps.items():
+                if where == place:
+                    pl.when(n == when)(step)
+
+        batch(n, hook, blocks, phi, psi, kern, w_ref, acc, xh, xl, yc, ye, z)
+
+    total = []
     for c in range(2):
-        for t in range(5):
-            x = acc[t, c * R:(c + 1) * R, :].reshape(24, 8, 128)
-            out_ref[c, t] = jnp.sum(x, axis=1)
-
-
-def compute(occ, psi, kern, w):
-    return pl.pallas_call(
-        local_kernel,
-        out_shape=jax.ShapeDtypeStruct((2, 5, 24, 128), F32),
-        in_specs=[pl.BlockSpec(memory_space=pltpu.VMEM)] * 4,
-        out_specs=pl.BlockSpec(memory_space=pltpu.VMEM),
-        scratch_shapes=SCRATCH,
-        compiler_params=pltpu.CompilerParams(vmem_limit_bytes=60 * 2**20),
-    )(occ, psi, kern, w)
-
-
-KPT_DEV = 2
-
-
-def spread_lanes(x, table):
-    y = jnp.dot(x.reshape(-1, 576), table, precision=lax.Precision.HIGHEST, preferred_element_type=F32)
-    return y.reshape(x.shape[:-1] + (5, 128))
+        total.append(jnp.concatenate(
+            [jnp.sum(acc[t, c * R:(c + 1) * R, :].reshape(24, 8, 128), axis=1) for t in range(5)], axis=1))
+    out_ref[...] = permute_exact(jnp.concatenate(total, axis=0), table[...], ((1,), (1,)))
+
+    for copy in first + second:
+        copy.wait_send()
+    for target in sent:
+        pltpu.make_async_remote_copy(
+            src_ref=blocks.at[0, pl.ds(0, 15)], dst_ref=blocks.at[target, pl.ds(0, 15)],
+            send_sem=band_send.at[target], recv_sem=band_recv.at[target],
+            device_id=sibling, device_id_type=MESH).wait_send()
 
 
 def shards(targets, occupied, kernels, partner, kernel_index):
-    per_kpoint = lax.axis_size("band") // KPT_DEV
-    my_group = lax.axis_index("ka")
-    kpoint = my_group * KPT_DEV + lax.axis_index("band") // per_kpoint
-    table = jnp.asarray(spread_table())
-    tables = jnp.asarray(half_tables())
-    mine = jnp.dot(
-        occupied.reshape(48, 576), table.astype(BF), preferred_element_type=F32
-    ).astype(BF).reshape(1, 2, 24, 640)
-    everyone = lax.all_gather(mine, "ka", axis=0, tiled=True)
-    partner_group = partner[my_group]
-    visitor = lax.dynamic_slice_in_dim(everyone, partner_group, 1, 0)
-    occ = lax.all_gather(visitor, "band", axis=0, tiled=True)
-    psi = spread_lanes(targets[0], table).transpose(0, 2, 1, 3)
-    pair = lax.dynamic_slice(kernel_index, (kpoint, partner_group * KPT_DEV), (1, KPT_DEV))[0]
-    kern = spread_lanes(kernels[pair] * (-1.0 / 13824.0), table).transpose(0, 2, 1, 3)
-    out = compute(occ, psi, kern, tables)
-    out = out.transpose(0, 2, 1, 3).reshape(48, 640)
-    out = jnp.dot(out, table.T, precision=lax.Precision.HIGHEST, preferred_element_type=F32)
+    vmem = pl.BlockSpec(memory_space=pltpu.VMEM)
+    smem = pl.BlockSpec(memory_space=pltpu.SMEM)
+    hbm = pl.BlockSpec(memory_space=pl.ANY)
+    sems = pltpu.SemaphoreType.DMA
+    out = pl.pallas_call(
+        whole_kernel,
+        out_shape=jax.ShapeDtypeStruct((48, 576), F32),
+        in_specs=[smem, smem, vmem, vmem, hbm, hbm, hbm],
+        out_specs=vmem,
+        scratch_shapes=[
+            pltpu.VMEM((5, 2 * R, 128), F32),
+            pltpu.VMEM((5, 2 * R, 128), BF),
+            pltpu.VMEM((5, 2 * R, 128), BF),
+            pltpu.VMEM((4, 2 * R, 128), F32),
+            pltpu.VMEM((4, 2 * R, 128), F32),
+            pltpu.VMEM((5, 2 * R, 128), F32),
+            pltpu.VMEM((5, 8 * 48, 128), F32),
+            pltpu.VMEM((5, 48, 128), F32),
+            pltpu.VMEM((5, 48, 128), F32),
+            pltpu.VMEM((4, 512, 256), BF),
+            pltpu.VMEM((576, 640), BF),
+            pltpu.VMEM((16, 24, 576), F32),
+            pltpu.VMEM((16, 16, 128), BF),
+            pltpu.VMEM((8, 2, 16, 128), BF),
+            pltpu.VMEM((8, 2, 16, 128), BF),
+            pltpu.VMEM((32, 16, 16, 128), BF),
+            sems((3,)), sems((8,)), sems((8,)), sems((8,)), sems((8,)), sems((32,)), sems((32,)),
+        ],
+        compiler_params=pltpu.CompilerParams(
+            vmem_limit_bytes=56 * 2**20, collective_id=0, has_side_effects=True),
+    )(
+        partner, kernel_index, occupied.reshape(48, 576), targets.reshape(48, 576), kernels,
+        jnp.asarray(spread_table().astype(ml_dtypes.bfloat16)), jnp.asarray(half_tables()),
+    )
     return out.reshape(1, 2, 24, 576)
 
 

time: 147 us -> 53.2 us (0.36)
  waiting for transfers between devices: 68.1 us -> 0 us
  blocking collectives: 30 us -> 0 us
  Pallas kernels: 21.9 us -> 51.5 us
  between operations: 16.1 us -> 0.01 us
  matrix products: 7.63 us -> 0 us
    all_gather x1 -> x0, waiting for transfers between devices: 68.1 us -> none  [shards(): occ = lax.all_gather(visitor, 'band', axis=0, tiled=True)]
    all_gather x1 -> x0, blocking collectives: 30 us -> none  [shards(): everyone = lax.all_gather(mine, 'ka', axis=0, tiled=True)]
    pallas_call x1, Pallas kernels: 21.9 us -> 51.5 us  [shards(): pl.pallas_call(whole_kernel, out_shape=jax.ShapeDtypeStruct((48, 576), F3...]
    dot_general x4 -> x0, matrix products: 7.63 us -> none  [the longest x2 3.23 us: spread_lanes(): jnp.dot(x.reshape(-1, 576), table, precision=lax.Precision.HIGHEST, prefe...]
    dynamic_slice x2 -> x0, local copies, waits for them, and re-layouts: 2.02 us -> none  [the longest x1 1.39 us: shards(): partner_group = partner[my_group]]
    unnamed x8 -> x1, local copies, waits for them, and re-layouts: 0.02 us -> 1.56 us
  transfers between devices with their start and end apart: 1 -> 0, of which waited for: 1 -> 0; matrix products, arithmetic and copies ran while one was open for 3% -> 0% of each run, Pallas kernels for 0% -> 0%
where the time goes in v2:
time: 53.2 us; the launch traced here: 53.1 us
  Pallas kernels  51.5 us (97%)
  local copies, waits for them, and re-layouts  1.56 us (3%)
    pallas_call x1, Pallas kernels, shards(): pl.pallas_call(whole_kernel, out_shape=jax.ShapeDtypeStruct((48, 576), F3...  51.5 us
    unnamed x1, local copies, waits for them, and re-layouts  1.56 us

profile of v2, /device:TPU:1, one launch (start us, length us, event | category | flops | bytes accessed | tf_op | source)
XLA Modules:
  0.0 53.1 jit_solution(12282233060570730849)
XLA Ops:
  0.0 51.5 %shard_map.73 = f32[48,576]{1,0:T(8,128)} custom-call(s32[8]{0:T(128)} %partner_ref.1, s32[16,16]{1,0:T(8,128)} %index_ref.1, bf16[48,576]{1,0:T(8,128)(2,1)} %bitcast.5, f32[48,576]{1,0:T(8,128)} %bitcast.4, f32[16,24,576]{2,1,0:T(8,128)} %kernels_hbm.1, bf16[576,640]{1,0:T(8,128)(2,1)} %constant.4.clone.table_hbm, bf16[4,512,256]{2,1,0:T(8,128)(2,1)} %constant.5.clone.w_hbm), custom_call_target="tpu_custom_call" | custom-call | tf_op jit(solution)/shard_map/pallas_call | solution.py:442
  51.5 1.6 %copy.9 = f32[1,2,24,576]{3,2,1,0:T(8,128)} copy(f32[1,2,24,576]{3,2,1,0:T(8,128)} %bitcast.3) | data formatting | bytes 221184

commit v3 on v1

v3 whole, which is shorter than its diff:
```python
import functools
import numpy as np
import ml_dtypes
import jax
import jax.numpy as jnp
from jax import lax
from jax.experimental import pallas as pl
from jax.experimental.pallas import tpu as pltpu

G = 24
H = 11
BF = jnp.bfloat16
F32 = jnp.float32


def point_order():
    order = np.full((5, 128), -1, np.int64)
    for t, (sb, sc) in enumerate(((1, 1), (1, -1), (-1, 1), (-1, -1))):
        for b in range(1, 12):
            for c in range(1, 12):
                order[t, (b - 1) * H + c - 1] = (sb * b % G) * G + sc * c % G
    edge = [b * G + c for b in range(G) for c in range(G) if b % 12 == 0 or c % 12 == 0]
    order[4, : len(edge)] = edge
    return order


def half_tables():
    order = point_order()
    core, edge = order[0], order[4]
    rows = np.concatenate([core, edge])
    live = rows >= 0
    b, c = rows // G, rows % G
    theta = 2 * np.pi * (np.outer(b, b) % G) / G
    phi = 2 * np.pi * (np.outer(c, c) % G) / G
    both = 2 * np.pi * ((np.outer(b, b) + np.outer(c, c)) % G) / G
    tables = np.stack([
        np.cos(theta) * np.cos(phi),
        np.cos(theta) * np.sin(phi),
        np.sin(theta) * np.cos(phi),
        -np.sin(theta) * np.sin(phi),
    ])
    tables[0, 128:, 128:] = np.cos(both)[128:, 128:]
    tables[1, 128:, 128:] = np.sin(both)[128:, 128:]
    tables[2:, 128:, 128:] = 0.0
    tables = tables * live[None, :, None] * live[None, None, :]
    high = tables.astype(ml_dtypes.bfloat16)
    low = (tables - high.astype(np.float64)).astype(ml_dtypes.bfloat16)
    return np.concatenate([high, low], axis=1)


def spread_table():
    order = point_order().reshape(-1)
    table = np.zeros((576, 640), np.float32)
    for lane, point in enumerate(order):
        if point >= 0:
            table[point, lane] = 1.0
    return table


def fft3(x, s3):
    (ar, ai), (br, bi), (cr, ci) = x
    tr, ti = br + cr, bi + ci
    dr, di = (br - cr) * s3, (bi - ci) * s3
    mr, mi = ar - 0.5 * tr, ai - 0.5 * ti
    return [(ar + tr, ai + ti), (mr + di, mi - dr), (mr - di, mi + dr)]


def add(x, y):
    return (x[0] + y[0], x[1] + y[1])


def sub(x, y):
    return (x[0] - y[0], x[1] - y[1])


def minus_i(x):
    return (x[1], -x[0])


def fft4(x):
    e0, e1 = add(x[0], x[2]), sub(x[0], x[2])
    o0, o1 = add(x[1], x[3]), sub(x[1], x[3])
    return [add(e0, o0), (e1[0] + o1[1], e1[1] - o1[0]), sub(e0, o0), (e1[0] - o1[1], e1[1] + o1[0])]


def fft8(x):
    r = float(np.sqrt(0.5))
    e = fft4([x[0], x[2], x[4], x[6]])
    o = fft4([x[1], x[3], x[5], x[7]])
    o1 = ((o[1][0] + o[1][1]) * r, (o[1][1] - o[1][0]) * r)
    o3 = ((o[3][1] - o[3][0]) * r, (o[3][0] + o[3][1]) * r)
    out = [None] * 8
    out[0], out[4] = add(e[0], o[0]), sub(e[0], o[0])
    out[1], out[5] = add(e[1], o1), sub(e[1], o1)
    out[2], out[6] = (e[2][0] + o[2][1], e[2][1] - o[2][0]), (e[2][0] - o[2][1], e[2][1] + o[2][0])
    out[3], out[7] = (e[3][0] + o3[0], e[3][1] - o3[1]), (e[3][0] - o3[0], e[3][1] + o3[1])
    return out


def fft24(load, store):
    s3 = float(np.sqrt(0.75))
    cols = []
    for n2 in range(8):
        cols.append(fft3([load((8 * n1 + 3 * n2) % 24) for n1 in range(3)], s3))
    for k1 in range(3):
        outs = fft8([cols[n2][k1] for n2 in range(8)])
        for k2 in range(8):
            k = next(k for k in range(24) if k % 3 == k1 and k % 8 == k2)
            store(k, outs[k2])


def split(x):
    high = x.astype(BF)
    return high, (x - high.astype(F32)).astype(BF)


R = 192


def rows(a, n=8):
    return pl.ds(pl.multiple_of(a * 8, 8), n)


def irows(a, n=8):
    return pl.ds(pl.multiple_of(R + a * 8, 8), n)


def batch(n, hook, blocks, phi, psi, kern, w_ref, acc, xh, xl, yc, ye, z):
    late = n // 2
    which = late * (4 - n)
    low = late * (3 - n)
    high = 1 - late * (n - 2)

    @pl.when(n < 3)
    def _():
        @pl.loop(0, 8)
        def _(j):
            from_slot = (1 - late) * (n * 4 + lax.rem(j, 4)) + late * (8 + j)
            for r in range(3):
                for t in range(5):
                    at = pl.ds(pl.multiple_of(j * 48 + r * 16, 16), 16)
                    phi[t, at, :] = blocks[from_slot, r * 5 + t].astype(F32)

    def orbital(c, t, a):
        return phi[t, pl.ds(c * 24 + a, 8, stride=48), :]

    upper = lax.broadcasted_iota(jnp.int32, (8, 128), 0) < 4

    def both(ref, t, a):
        first = jnp.broadcast_to(ref[low, t, pl.ds(a, 1), :], (8, 128))
        second = jnp.broadcast_to(ref[high, t, pl.ds(a, 1), :], (8, 128))
        return jnp.where(upper, first, second)

    def density(t, a):
        pr, pi = orbital(0, t, a), orbital(1, t, a)
        tr, ti = both(psi, t, a), both(psi, t, 24 + a)
        return pr * tr + pi * ti, pr * ti - pi * tr

    @pl.loop(0, 6)
    def _(hh):
        for h in (2 * hh, 2 * hh + 1):
            grid = []
            for t in range(5):
                lo = density(t, 2 * h)
                hi = density(t, 2 * h + 1)
                grid.append([jnp.concatenate([lo[c], hi[c]], axis=0) for c in range(2)])
            for c in range(2):
                pp, pm, mp, mm, edge = (grid[t][c] for t in range(5))
                s, d, u, v = pp + mm, pp - mm, pm + mp, pm - mp
                at = pl.ds(pl.multiple_of(c * R + h * 16, 16), 16)
                for p, x in enumerate((s + u, d - v, d + v, s - u, edge)):
                    xh[p, at, :], xl[p, at, :] = split(x)

    hook(0)

    def product(p):
        left = jnp.concatenate([xh[p], xh[4], xh[p], xh[4], xl[p], xl[4]], axis=1)
        right = jnp.concatenate([w_ref[p], w_ref[p, :256]], axis=0)
        y = jnp.dot(left, right, preferred_element_type=F32)
        yc[p] = y[:, :128]
        ye[p] = y[:, 128:]

    def edge_sum(a):
        er = ye[0, rows(a), :] + ye[3, rows(a), :]
        ei = ye[0, irows(a), :] + ye[3, irows(a), :]
        xr = ye[1, rows(a), :] + ye[2, rows(a), :]
        xi = ye[1, irows(a), :] + ye[2, irows(a), :]
        return er, ei, xr, xi

    def forward_edge(a):
        er, ei, xr, xi = edge_sum(a)
        return er + xi, ei - xr

    def keep(p):
        def store(k, x):
            z[p, rows(k), :] = x[0]
            z[p, irows(k), :] = x[1]
        return store

    for p in range(4):
        product(p)
        fft24(lambda a: (yc[p, rows(a), :], yc[p, irows(a), :]), keep(p))
    fft24(forward_edge, keep(4))
    hook(1)

    @pl.loop(0, 12)
    def _(aa):
        for a in (2 * aa, 2 * aa + 1):
            re = [z[p, rows(a), :] for p in range(5)]
            im = [z[p, irows(a), :] for p in range(5)]
            k = [both(kern, t, a) for t in range(5)]
            pr, qr = re[0] + re[3], re[0] - re[3]
            pi, qi = im[0] + im[3], im[0] - im[3]
            sr, dr = re[2] + re[1], re[2] - re[1]
            si, di = im[2] + im[1], im[2] - im[1]
            for out, (pp, mm, pm, mp) in enumerate((
                (pr + si, pr - si, qr + di, qr - di),
                (pi - sr, pi + sr, qi - dr, qi + dr),
            )):
                pp, pm, mp, mm = pp * k[0], pm * k[1], mp * k[2], mm * k[3]
                s, d, u, v = pp + mm, pp - mm, pm + mp, pm - mp
                at = irows(a) if out else rows(a)
                for p, x in enumerate((s + u, d - v, d + v, s - u)):
                    z[p, at, :] = x
            z[4, rows(a), :] = re[4] * k[4]
            z[4, irows(a), :] = im[4] * k[4]

    hook(2)

    for p in (4, 0, 1, 2, 3):
        got = {}

        def store(k, x):
            got[k] = x

        fft24(lambda a: (z[p, irows(a), :], z[p, rows(a), :]), store)
        for h in range(12):
            for c in range(2):
                x = jnp.concatenate([got[2 * h][1 - c], got[2 * h + 1][1 - c]], axis=0)
                at = pl.ds(c * R + h * 16, 16)
                xh[p, at, :], xl[p, at, :] = split(x)
        if p < 4:
            product(p)
    hook(3)

    @pl.loop(0, 8)
    def _(aa):
        for a in (3 * aa, 3 * aa + 1, 3 * aa + 2):
            re = [yc[p, rows(a), :] for p in range(4)]
            im = [yc[p, irows(a), :] for p in range(4)]
            pr, qr = re[0] + re[3], re[0] - re[3]
            pi, qi = im[0] + im[3], im[0] - im[3]
            sr, dr = re[2] + re[1], re[2] - re[1]
            si, di = im[2] + im[1], im[2] - im[1]
            er, ei, xr, xi = edge_sum(a)
            vr = (pr - si, qr - di, qr + di, pr + si, er - xi)
            vi = (pi + sr, qi + dr, qi - dr, pi - sr, ei + xr)
            for t in range(5):
                fr, fi = orbital(0, t, a), orbital(1, t, a)
                acc[which, t, rows(a), :] += fr * vr[t] - fi * vi[t]
                acc[which, t, irows(a), :] += fr * vi[t] + fi * vr[t]

    hook(4)


MESH = pl.DeviceIdType.MESH
FULL = (((1,), (0,)), ((), ()))


def permute_exact(x, table):
    high = x.astype(BF)
    rest = x - high.astype(F32)
    mid = rest.astype(BF)
    low = (rest - mid.astype(F32)).astype(BF)
    y = jnp.dot(jnp.concatenate([high, mid, low], axis=0), table, preferred_element_type=F32)
    m = x.shape[0]
    return y[:m] + y[m:2 * m] + y[2 * m:]


def whole_kernel(partner_ref, index_ref, occ_ref, tgt_ref, kernels_hbm, table_hbm, back_hbm, w_hbm, out_ref,
                 acc, xh, xl, yc, ye, z, phi, psi, kern, w_ref, table, back, kernels, far, part, came,
                 mine, everyone, blocks,
                 load_sem, one_send, one_recv, pair_send, pair_recv, band_send, band_recv):
    me = lax.axis_index("ka")
    band = lax.axis_index("band")
    core = lax.rem(band, 2)
    zed = lax.rem(band // 2, 8)
    why = band // 16

    def flip(d):
        out = 0
        for bit in (1, 2, 4):
            have = lax.rem(zed // bit, 2)
            out = out + bit * ((1 - have) if d & bit else have)
        return out

    along = {d: (me, why * 16 + flip(d) * 2 + core) for d in (1, 2, 3, 7)}
    across = (me, (1 - why) * 16 + zed * 2 + core)
    sibling = (me, band + 1 - 2 * core)
    peers = list(along.values()) + [across, sibling]

    loads = [
        pltpu.make_async_copy(table_hbm, table, load_sem.at[0]),
        pltpu.make_async_copy(w_hbm, w_ref, load_sem.at[1]),
        pltpu.make_async_copy(kernels_hbm, kernels, load_sem.at[2]),
        pltpu.make_async_copy(back_hbm, back, load_sem.at[3]),
    ]
    for load in loads:
        load.start()

    barrier = pltpu.get_barrier_semaphore()
    for k in range(1, 8):
        pl.semaphore_signal(barrier, inc=1, device_id=(lax.rem(me + k, 8), band), device_id_type=MESH)
    for peer in peers:
        pl.semaphore_signal(barrier, inc=1, device_id=peer, device_id_type=MESH)

    loads[0].wait()
    own = jnp.dot(occ_ref[...], table[...], preferred_element_type=F32).astype(BF)
    for r in range(3):
        for t in range(5):
            mine[r * 5 + t] = own[r * 16:(r + 1) * 16, t * 128:(t + 1) * 128]
    everyone[me] = mine[...]

    def set_psi(which, field):
        y = permute_exact(field, table[...])
        for t in range(5):
            psi[which, t] = y[:, t * 128:(t + 1) * 128]

    set_psi(0, tgt_ref[...])
    acc[...] = jnp.zeros_like(acc)
    pl.semaphore_wait(barrier, 7 + len(peers))

    def remote(src, dst, send_sem, recv_sem, peer):
        return pltpu.make_async_remote_copy(
            src_ref=src, dst_ref=dst, send_sem=send_sem, recv_sem=recv_sem, device_id=peer, device_id_type=MESH)

    first = [
        remote(mine, everyone.at[me], one_send.at[k], one_recv.at[k], (lax.rem(me + k, 8), band))
        for k in range(1, 8)]
    for copy in first:
        copy.start()
    swap = remote(tgt_ref, far, pair_send.at[0], pair_recv.at[0], across)
    swap.start()

    loads[2].wait()
    group = partner_ref[me]
    scaled = jnp.concatenate(
        [kernels[index_ref[me * 2 + k, group * 2 + why]] for k in (why, 1 - why)], axis=0) * (-1.0 / 13824.0)
    kern_all = permute_exact(scaled, table[...])
    for k in range(2):
        for t in range(5):
            kern[k, t] = kern_all[k * 24:(k + 1) * 24, t * 128:(t + 1) * 128]
    loads[1].wait()
    loads[3].wait()

    sent = []

    def moved(target):
        return remote(blocks.at[0], blocks.at[target], band_send.at[target], band_recv.at[target], sibling)

    def send(source, target, peer):
        remote(blocks.at[source], blocks.at[target], band_send.at[target], band_recv.at[target], peer).start()
        sent.append(target)

    def take(*chips):
        for d in chips:
            moved(2 * d).wait_recv()
            send(2 * d, 2 * d + 1, sibling)
            if d == 7:
                for e in (1, 2, 3):
                    send(14, 2 * (7 - e), along[e])

    def need(*chips):
        for d in chips:
            moved(2 * d + 1).wait_recv()

    for copy in first:
        copy.wait_recv()
    blocks[0] = everyone[partner_ref[me]]
    send(0, 1, sibling)
    for d in (1, 7, 2, 3):
        send(0, 2 * d, along[d])

    swap.wait_recv()
    set_psi(1, far[...])
    take(1)
    need(0, 1)

    def total(part_of):
        sums = []
        for c in range(2):
            tiles = []
            for t in range(5):
                x = part_of(t, c)
                tiles.append(jnp.sum(x.reshape(24, 8, 128), axis=1))
            sums.append(jnp.concatenate(tiles, axis=1))
        return jnp.concatenate(sums, axis=0)

    sub = lax.rem(lax.broadcasted_iota(jnp.int32, (R, 128), 0), 8)
    back_copy = remote(part, came, pair_send.at[1], pair_recv.at[1], across)

    def give_back():
        part[...] = total(lambda t, c: acc[2, t, c * R:(c + 1) * R, :] + jnp.where(sub < 4, 0.0, acc[0, t, c * R:(c + 1) * R, :]))
        back_copy.start()

    steps = {
        (0, 0): lambda: take(2),
        (0, 1): lambda: take(3),
        (0, 3): lambda: take(7),
        (0, 4): lambda: need(2, 3),
        (1, 0): lambda: take(6),
        (1, 1): lambda: take(5),
        (1, 3): lambda: take(4),
        (1, 4): lambda: need(4, 5, 6, 7),
        (2, 4): give_back,
    }

    @pl.loop(0, 4)
    def _(n):
        def hook(place):
            for (when, where), step in steps.items():
                if where == place:
                    pl.when(n == when)(step)

        batch(n, hook, blocks, phi, psi, kern, w_ref, acc, xh, xl, yc, ye, z)

    mixed = total(lambda t, c: acc[1, t, c * R:(c + 1) * R, :] + jnp.where(sub < 4, acc[0, t, c * R:(c + 1) * R, :], 0.0))
    back_copy.wait_recv()
    out_ref[...] = permute_exact(mixed + came[...], back[...])

    for copy in first + [swap, back_copy]:
        copy.wait_send()
    for target in sent:
        moved(target).wait_send()


def shards(targets, occupied, kernels, partner, kernel_index):
    vmem = pl.BlockSpec(memory_space=pltpu.VMEM)
    smem = pl.BlockSpec(memory_space=pltpu.SMEM)
    hbm = pl.BlockSpec(memory_space=pl.ANY)
    sems = pltpu.SemaphoreType.DMA
    table = spread_table().astype(ml_dtypes.bfloat16)
    out = pl.pallas_call(
        whole_kernel,
        out_shape=jax.ShapeDtypeStruct((48, 576), F32),
        in_specs=[smem, smem, vmem, vmem, hbm, hbm, hbm, hbm],
        out_specs=vmem,
        scratch_shapes=[
            pltpu.VMEM((3, 5, 2 * R, 128), F32),
            pltpu.VMEM((5, 2 * R, 128), BF),
            pltpu.VMEM((5, 2 * R, 128), BF),
            pltpu.VMEM((4, 2 * R, 128), F32),
            pltpu.VMEM((4, 2 * R, 128), F32),
            pltpu.VMEM((5, 2 * R, 128), F32),
            pltpu.VMEM((5, 8 * 48, 128), F32),
            pltpu.VMEM((2, 5, 48, 128), F32),
            pltpu.VMEM((2, 5, 24, 128), F32),
            pltpu.VMEM((4, 512, 256), BF),
            pltpu.VMEM((576, 640), BF),
            pltpu.VMEM((640, 576), BF),
            pltpu.VMEM((16, 24, 576), F32),
            pltpu.VMEM((48, 576), F32),
            pltpu.VMEM((48, 640), F32),
            pltpu.VMEM((48, 640), F32),
            pltpu.VMEM((15, 16, 128), BF),
            pltpu.VMEM((8, 15, 16, 128), BF),
            pltpu.VMEM((16, 15, 16, 128), BF),
            sems((4,)), sems((8,)), sems((8,)), sems((2,)), sems((2,)), sems((16,)), sems((16,)),
        ],
        compiler_params=pltpu.CompilerParams(
            vmem_limit_bytes=56 * 2**20, collective_id=0, has_side_effects=True),
    )(
        partner, kernel_index, occupied.reshape(48, 576), targets.reshape(48, 576), kernels,
        jnp.asarray(table), jnp.asarray(np.ascontiguousarray(table.T)), jnp.asarray(half_tables()),
    )
    return out.reshape(1, 2, 24, 576)


def solution(mesh):
    from jax.sharding import PartitionSpec as P
    return jax.shard_map(
        shards,
        mesh=mesh,
        in_specs=(P(("ka", "band"), None, None, None), P(("ka", "band"), None, None, None), P(), P(), P()),
        out_specs=P(("ka", "band"), None, None, None),
        check_vma=False,
    )
```

time: 147 us -> 45.7 us (0.31)
  waiting for transfers between devices: 68.1 us -> 0 us
  blocking collectives: 30 us -> 0 us
  Pallas kernels: 21.9 us -> 44 us
  between operations: 16.1 us -> 0.01 us
  matrix products: 7.63 us -> 0 us
    all_gather x1 -> x0, waiting for transfers between devices: 68.1 us -> none  [shards(): occ = lax.all_gather(visitor, 'band', axis=0, tiled=True)]
    all_gather x1 -> x0, blocking collectives: 30 us -> none  [shards(): everyone = lax.all_gather(mine, 'ka', axis=0, tiled=True)]
    pallas_call x1, Pallas kernels: 21.9 us -> 44 us  [shards(): pl.pallas_call(whole_kernel, out_shape=jax.ShapeDtypeStruct((48, 576), F3...]
    dot_general x4 -> x0, matrix products: 7.63 us -> none  [the longest x2 3.23 us: spread_lanes(): jnp.dot(x.reshape(-1, 576), table, precision=lax.Precision.HIGHEST, prefe...]
    dynamic_slice x2 -> x0, local copies, waits for them, and re-layouts: 2.02 us -> none  [the longest x1 1.39 us: shards(): partner_group = partner[my_group]]
    unnamed x8 -> x1, local copies, waits for them, and re-layouts: 0.02 us -> 1.56 us
  transfers between devices with their start and end apart: 1 -> 0, of which waited for: 1 -> 0; matrix products, arithmetic and copies ran while one was open for 3% -> 0% of each run, Pallas kernels for 0% -> 0%
where the time goes in v3:
time: 45.7 us; the launch traced here: 45.6 us
  Pallas kernels  44 us (96%)
  local copies, waits for them, and re-layouts  1.56 us (3%)
    pallas_call x1, Pallas kernels, shards(): pl.pallas_call(whole_kernel, out_shape=jax.ShapeDtypeStruct((48, 576), F3...  44 us
    unnamed x1, local copies, waits for them, and re-layouts  1.56 us

profile of v3, /device:TPU:1, one launch (start us, length us, event | category | flops | bytes accessed | tf_op | source)
XLA Modules:
  0.0 45.6 jit_solution(8459280743227969768)
XLA Ops:
  0.0 44.0 %shard_map.82 = f32[48,576]{1,0:T(8,128)} custom-call(s32[8]{0:T(128)} %partner_ref.1, s32[16,16]{1,0:T(8,128)} %index_ref.1, bf16[48,576]{1,0:T(8,128)(2,1)} %bitcast.5, f32[48,576]{1,0:T(8,128)} %bitcast.4, f32[16,24,576]{2,1,0:T(8,128)} %kernels_hbm.1, bf16[576,640]{1,0:T(8,128)(2,1)} %constant.6.clone.table_hbm, ...), custom_call_target="tpu_custom_call" | custom-call | tf_op jit(solution)/shard_map/pallas_call | solution.py:443
  44.0 1.6 %copy.10 = f32[1,2,24,576]{3,2,1,0:T(8,128)} copy(f32[1,2,24,576]{3,2,1,0:T(8,128)} %bitcast.3) | data formatting | bytes 221184

commit v4 on v3

--- a/solution.py
+++ b/solution.py
@@ -45,7 +45,12 @@
     tables = tables * live[None, :, None] * live[None, None, :]
     high = tables.astype(ml_dtypes.bfloat16)
     low = (tables - high.astype(np.float64)).astype(ml_dtypes.bfloat16)
-    return np.concatenate([high, low], axis=1)
+    tables = np.concatenate([high, low], axis=1)
+    last = np.concatenate([high[3, :128, :128], low[3, :128, :128]], axis=1)
+    tables[3] = 0
+    tables[3, :128] = last
+    tables[3, 128:256, :128] = last[:, :128]
+    return tables
 
 
 def spread_table():
@@ -127,9 +132,7 @@
 
 def batch(n, hook, blocks, phi, psi, kern, w_ref, acc, xh, xl, yc, ye, z):
     late = n // 2
-    which = late * (4 - n)
-    low = late * (3 - n)
-    high = 1 - late * (n - 2)
+    kind = late * (n - 1)
 
     @pl.when(n < 3)
     def _():
@@ -144,21 +147,14 @@
     def orbital(c, t, a):
         return phi[t, pl.ds(c * 24 + a, 8, stride=48), :]
 
-    upper = lax.broadcasted_iota(jnp.int32, (8, 128), 0) < 4
-
-    def both(ref, t, a):
-        first = jnp.broadcast_to(ref[low, t, pl.ds(a, 1), :], (8, 128))
-        second = jnp.broadcast_to(ref[high, t, pl.ds(a, 1), :], (8, 128))
-        return jnp.where(upper, first, second)
-
     def density(t, a):
         pr, pi = orbital(0, t, a), orbital(1, t, a)
-        tr, ti = both(psi, t, a), both(psi, t, 24 + a)
+        tr, ti = psi[kind, t, rows(a), :], psi[kind, t, irows(a), :]
         return pr * tr + pi * ti, pr * ti - pi * tr
 
-    @pl.loop(0, 6)
+    @pl.loop(0, 4)
     def _(hh):
-        for h in (2 * hh, 2 * hh + 1):
+        for h in (3 * hh, 3 * hh + 1, 3 * hh + 2):
             grid = []
             for t in range(5):
                 lo = density(t, 2 * h)
@@ -174,6 +170,11 @@
     hook(0)
 
     def product(p):
+        if p == 3:
+            left = jnp.concatenate([xh[3], xl[3]], axis=1)
+            y = jnp.dot(left, w_ref[3, :256], preferred_element_type=F32)
+            yc[3] = y[:, :128] + y[:, 128:]
+            return
         left = jnp.concatenate([xh[p], xh[4], xh[p], xh[4], xl[p], xl[4]], axis=1)
         right = jnp.concatenate([w_ref[p], w_ref[p, :256]], axis=0)
         y = jnp.dot(left, right, preferred_element_type=F32)
@@ -181,11 +182,9 @@
         ye[p] = y[:, 128:]
 
     def edge_sum(a):
-        er = ye[0, rows(a), :] + ye[3, rows(a), :]
-        ei = ye[0, irows(a), :] + ye[3, irows(a), :]
         xr = ye[1, rows(a), :] + ye[2, rows(a), :]
         xi = ye[1, irows(a), :] + ye[2, irows(a), :]
-        return er, ei, xr, xi
+        return ye[0, rows(a), :], ye[0, irows(a), :], xr, xi
 
     def forward_edge(a):
         er, ei, xr, xi = edge_sum(a)
@@ -203,12 +202,12 @@
     fft24(forward_edge, keep(4))
     hook(1)
 
-    @pl.loop(0, 12)
+    @pl.loop(0, 4)
     def _(aa):
-        for a in (2 * aa, 2 * aa + 1):
+        for a in (6 * aa + i for i in range(6)):
             re = [z[p, rows(a), :] for p in range(5)]
             im = [z[p, irows(a), :] for p in range(5)]
-            k = [both(kern, t, a) for t in range(5)]
+            k = [kern[kind, t, rows(a), :] for t in range(5)]
             pr, qr = re[0] + re[3], re[0] - re[3]
             pi, qi = im[0] + im[3], im[0] - im[3]
             sr, dr = re[2] + re[1], re[2] - re[1]
@@ -231,34 +230,36 @@
         got = {}
 
         def store(k, x):
-            got[k] = x
+            place = k % 3 * 8 + k % 8
+            got[place] = x
+            if place % 2:
+                for c in range(2):
+                    y = jnp.concatenate([got[place - 1][1 - c], x[1 - c]], axis=0)
+                    at = pl.ds(c * R + place // 2 * 16, 16)
+                    xh[p, at, :], xl[p, at, :] = split(y)
 
         fft24(lambda a: (z[p, irows(a), :], z[p, rows(a), :]), store)
-        for h in range(12):
-            for c in range(2):
-                x = jnp.concatenate([got[2 * h][1 - c], got[2 * h + 1][1 - c]], axis=0)
-                at = pl.ds(c * R + h * 16, 16)
-                xh[p, at, :], xl[p, at, :] = split(x)
         if p < 4:
             product(p)
     hook(3)
 
-    @pl.loop(0, 8)
+    @pl.loop(0, 4)
     def _(aa):
-        for a in (3 * aa, 3 * aa + 1, 3 * aa + 2):
-            re = [yc[p, rows(a), :] for p in range(4)]
-            im = [yc[p, irows(a), :] for p in range(4)]
+        for a in (6 * aa + i for i in range(6)):
+            b = lax.rem(a, 3) * 8 + lax.rem(a, 8)
+            re = [yc[p, rows(b), :] for p in range(4)]
+            im = [yc[p, irows(b), :] for p in range(4)]
             pr, qr = re[0] + re[3], re[0] - re[3]
             pi, qi = im[0] + im[3], im[0] - im[3]
             sr, dr = re[2] + re[1], re[2] - re[1]
             si, di = im[2] + im[1], im[2] - im[1]
-            er, ei, xr, xi = edge_sum(a)
+            er, ei, xr, xi = edge_sum(b)
             vr = (pr - si, qr - di, qr + di, pr + si, er - xi)
             vi = (pi + sr, qi + dr, qi - dr, pi - sr, ei + xr)
             for t in range(5):
                 fr, fi = orbital(0, t, a), orbital(1, t, a)
-                acc[which, t, rows(a), :] += fr * vr[t] - fi * vi[t]
-                acc[which, t, irows(a), :] += fr * vi[t] + fi * vr[t]
+                acc[kind, t, rows(a), :] += fr * vr[t] - fi * vi[t]
+                acc[kind, t, irows(a), :] += fr * vi[t] + fi * vr[t]
 
     hook(4)
 
@@ -277,9 +278,9 @@
     return y[:m] + y[m:2 * m] + y[2 * m:]
 
 
-def whole_kernel(partner_ref, index_ref, occ_ref, tgt_ref, kernels_hbm, table_hbm, back_hbm, w_hbm, out_ref,
-                 acc, xh, xl, yc, ye, z, phi, psi, kern, w_ref, table, back, kernels, far, part, came,
-                 mine, everyone, blocks,
+def whole_kernel(partner_ref, index_ref, occ_hbm, tgt_hbm, kernels_hbm, table_hbm, back_hbm, w_hbm, out_ref,
+                 acc, xh, xl, yc, ye, z, phi, psi, kern, w_ref, table, back, kernels, tgt, far, part, came,
+                 everyone, blocks,
                  load_sem, one_send, one_recv, pair_send, pair_recv, band_send, band_recv):
     me = lax.axis_index("ka")
     band = lax.axis_index("band")
@@ -299,35 +300,18 @@
     sibling = (me, band + 1 - 2 * core)
     peers = list(along.values()) + [across, sibling]
 
-    loads = [
-        pltpu.make_async_copy(table_hbm, table, load_sem.at[0]),
-        pltpu.make_async_copy(w_hbm, w_ref, load_sem.at[1]),
-        pltpu.make_async_copy(kernels_hbm, kernels, load_sem.at[2]),
-        pltpu.make_async_copy(back_hbm, back, load_sem.at[3]),
-    ]
-    for load in loads:
-        load.start()
-
     barrier = pltpu.get_barrier_semaphore()
     for k in range(1, 8):
         pl.semaphore_signal(barrier, inc=1, device_id=(lax.rem(me + k, 8), band), device_id_type=MESH)
     for peer in peers:
         pl.semaphore_signal(barrier, inc=1, device_id=peer, device_id_type=MESH)
 
-    loads[0].wait()
-    own = jnp.dot(occ_ref[...], table[...], preferred_element_type=F32).astype(BF)
-    for r in range(3):
-        for t in range(5):
-            mine[r * 5 + t] = own[r * 16:(r + 1) * 16, t * 128:(t + 1) * 128]
-    everyone[me] = mine[...]
-
-    def set_psi(which, field):
-        y = permute_exact(field, table[...])
-        for t in range(5):
-            psi[which, t] = y[:, t * 128:(t + 1) * 128]
-
-    set_psi(0, tgt_ref[...])
-    acc[...] = jnp.zeros_like(acc)
+    loads = [
+        pltpu.make_async_copy(src, dst, load_sem.at[k]) for k, (src, dst) in enumerate((
+            (occ_hbm, everyone.at[me]), (tgt_hbm, tgt), (table_hbm, table),
+            (w_hbm, w_ref), (kernels_hbm, kernels), (back_hbm, back)))]
+    for load in loads:
+        load.start()
     pl.semaphore_wait(barrier, 7 + len(peers))
 
     def remote(src, dst, send_sem, recv_sem, peer):
@@ -335,23 +319,32 @@
             src_ref=src, dst_ref=dst, send_sem=send_sem, recv_sem=recv_sem, device_id=peer, device_id_type=MESH)
 
     first = [
-        remote(mine, everyone.at[me], one_send.at[k], one_recv.at[k], (lax.rem(me + k, 8), band))
+        remote(occ_hbm, everyone.at[me], one_send.at[k], one_recv.at[k], (lax.rem(me + k, 8), band))
         for k in range(1, 8)]
     for copy in first:
         copy.start()
-    swap = remote(tgt_ref, far, pair_send.at[0], pair_recv.at[0], across)
+    swap = remote(tgt_hbm, far, pair_send.at[0], pair_recv.at[0], across)
     swap.start()
 
-    loads[2].wait()
+    for load in loads:
+        load.wait()
+
+    def spread(refs, which, field):
+        for a in range(field.shape[0]):
+            for t in range(5):
+                x = jnp.broadcast_to(field[a:a + 1, t * 128:(t + 1) * 128], (8, 128))
+                refs[which, t, a * 8:(a + 1) * 8, :] = x
+                half = slice(a * 8, a * 8 + 4) if which == 2 else slice(a * 8 + 4, a * 8 + 8)
+                refs[0, t, half, :] = x[:4]
+
     group = partner_ref[me]
     scaled = jnp.concatenate(
         [kernels[index_ref[me * 2 + k, group * 2 + why]] for k in (why, 1 - why)], axis=0) * (-1.0 / 13824.0)
     kern_all = permute_exact(scaled, table[...])
-    for k in range(2):
-        for t in range(5):
-            kern[k, t] = kern_all[k * 24:(k + 1) * 24, t * 128:(t + 1) * 128]
-    loads[1].wait()
-    loads[3].wait()
+    spread(kern, 2, kern_all[:24])
+    spread(kern, 1, kern_all[24:])
+    spread(psi, 2, permute_exact(tgt[...], table[...]))
+    acc[...] = jnp.zeros_like(acc)
 
     sent = []
 
@@ -376,37 +369,44 @@
 
     for copy in first:
         copy.wait_recv()
-    blocks[0] = everyone[partner_ref[me]]
+    own = jnp.dot(everyone[group], table[...], preferred_element_type=F32).astype(BF)
+    for r in range(3):
+        for t in range(5):
+            blocks[0, r * 5 + t] = own[r * 16:(r + 1) * 16, t * 128:(t + 1) * 128]
     send(0, 1, sibling)
-    for d in (1, 7, 2, 3):
+    for d in (7, 1, 2, 3):
         send(0, 2 * d, along[d])
 
     swap.wait_recv()
-    set_psi(1, far[...])
+    spread(psi, 1, permute_exact(far[...], table[...]))
     take(1)
+    take(7)
     need(0, 1)
 
-    def total(part_of):
+    def total(kinds):
         sums = []
         for c in range(2):
-            tiles = []
-            for t in range(5):
-                x = part_of(t, c)
-                tiles.append(jnp.sum(x.reshape(24, 8, 128), axis=1))
-            sums.append(jnp.concatenate(tiles, axis=1))
+            for block in range(3):
+                tiles = []
+                for t in range(5):
+                    x = None
+                    for kind, subs in kinds:
+                        for s in subs:
+                            y = acc[kind, t, pl.ds(c * R + block * 64 + s, 8, stride=8), :]
+                            x = y if x is None else x + y
+                    tiles.append(x)
+                sums.append(jnp.concatenate(tiles, axis=1))
         return jnp.concatenate(sums, axis=0)
 
-    sub = lax.rem(lax.broadcasted_iota(jnp.int32, (R, 128), 0), 8)
     back_copy = remote(part, came, pair_send.at[1], pair_recv.at[1], across)
 
     def give_back():
-        part[...] = total(lambda t, c: acc[2, t, c * R:(c + 1) * R, :] + jnp.where(sub < 4, 0.0, acc[0, t, c * R:(c + 1) * R, :]))
+        part[...] = total(((0, range(4, 8)), (1, range(8))))
         back_copy.start()
 
     steps = {
         (0, 0): lambda: take(2),
         (0, 1): lambda: take(3),
-        (0, 3): lambda: take(7),
         (0, 4): lambda: need(2, 3),
         (1, 0): lambda: take(6),
         (1, 1): lambda: take(5),
@@ -424,7 +424,7 @@
 
         batch(n, hook, blocks, phi, psi, kern, w_ref, acc, xh, xl, yc, ye, z)
 
-    mixed = total(lambda t, c: acc[1, t, c * R:(c + 1) * R, :] + jnp.where(sub < 4, acc[0, t, c * R:(c + 1) * R, :], 0.0))
+    mixed = total(((0, range(4)), (2, range(8))))
     back_copy.wait_recv()
     out_ref[...] = permute_exact(mixed + came[...], back[...])
 
@@ -443,7 +443,7 @@
     out = pl.pallas_call(
         whole_kernel,
         out_shape=jax.ShapeDtypeStruct((48, 576), F32),
-        in_specs=[smem, smem, vmem, vmem, hbm, hbm, hbm, hbm],
+        in_specs=[smem, smem, hbm, hbm, hbm, hbm, hbm, hbm],
         out_specs=vmem,
         scratch_shapes=[
             pltpu.VMEM((3, 5, 2 * R, 128), F32),
@@ -453,19 +453,19 @@
             pltpu.VMEM((4, 2 * R, 128), F32),
             pltpu.VMEM((5, 2 * R, 128), F32),
             pltpu.VMEM((5, 8 * 48, 128), F32),
-            pltpu.VMEM((2, 5, 48, 128), F32),
-            pltpu.VMEM((2, 5, 24, 128), F32),
+            pltpu.VMEM((3, 5, 2 * R, 128), F32),
+            pltpu.VMEM((3, 5, R, 128), F32),
             pltpu.VMEM((4, 512, 256), BF),
             pltpu.VMEM((576, 640), BF),
             pltpu.VMEM((640, 576), BF),
             pltpu.VMEM((16, 24, 576), F32),
             pltpu.VMEM((48, 576), F32),
+            pltpu.VMEM((48, 576), F32),
             pltpu.VMEM((48, 640), F32),
             pltpu.VMEM((48, 640), F32),
-            pltpu.VMEM((15, 16, 128), BF),
-            pltpu.VMEM((8, 15, 16, 128), BF),
+            pltpu.VMEM((8, 48, 576), BF),
             pltpu.VMEM((16, 15, 16, 128), BF),
-            sems((4,)), sems((8,)), sems((8,)), sems((2,)), sems((2,)), sems((16,)), sems((16,)),
+            sems((6,)), sems((8,)), sems((8,)), sems((2,)), sems((2,)), sems((16,)), sems((16,)),
         ],
         compiler_params=pltpu.CompilerParams(
             vmem_limit_bytes=56 * 2**20, collective_id=0, has_side_effects=True),

time: 45.7 us -> 43.9 us (0.961)
  the two profiles are of different devices: /device:TPU:1 before, /device:TPU:7 now
where the time goes in v4:
time: 43.9 us; the launch traced here: 43.7 us
  Pallas kernels  42.1 us (96%)
  local copies, waits for them, and re-layouts  1.56 us (4%)
    pallas_call x1, Pallas kernels, shards(): pl.pallas_call(whole_kernel, out_shape=jax.ShapeDtypeStruct((48, 576), F3...  42.1 us
    unnamed x1, local copies, waits for them, and re-layouts  1.56 us

profile of v4, /device:TPU:7, one launch (start us, length us, event | category | flops | bytes accessed | tf_op | source)
XLA Modules:
  0.0 43.7 jit_solution(14084583122416245402)
XLA Ops:
  0.0 42.1 %shard_map.82 = f32[48,576]{1,0:T(8,128)} custom-call(s32[8]{0:T(128)} %partner_ref.1, s32[16,16]{1,0:T(8,128)} %index_ref.1, bf16[48,576]{1,0:T(8,128)(2,1)} %bitcast.5, f32[48,576]{1,0:T(8,128)} %bitcast.4, f32[16,24,576]{2,1,0:T(8,128)} %kernels_hbm.1, bf16[576,640]{1,0:T(8,128)(2,1)} %constant.6.clone.table_hbm, ...), custom_call_target="tpu_custom_call" | custom-call | tf_op jit(solution)/shard_map/pallas_call | solution.py:443
  42.2 1.6 %copy.10 = f32[1,2,24,576]{3,2,1,0:T(8,128)} copy(f32[1,2,24,576]{3,2,1,0:T(8,128)} %bitcast.3) | data formatting | bytes 221184

commit v5 on v4

--- a/solution.py
+++ b/solution.py
@@ -324,7 +324,6 @@
     for copy in first:
         copy.start()
     swap = remote(tgt_hbm, far, pair_send.at[0], pair_recv.at[0], across)
-    swap.start()
 
     for load in loads:
         load.wait()
@@ -369,17 +368,18 @@
 
     for copy in first:
         copy.wait_recv()
+    swap.start()
     own = jnp.dot(everyone[group], table[...], preferred_element_type=F32).astype(BF)
     for r in range(3):
         for t in range(5):
             blocks[0, r * 5 + t] = own[r * 16:(r + 1) * 16, t * 128:(t + 1) * 128]
-    send(0, 1, sibling)
     for d in (7, 1, 2, 3):
         send(0, 2 * d, along[d])
-
+    send(0, 1, sibling)
+
+    take(1)
     swap.wait_recv()
     spread(psi, 1, permute_exact(far[...], table[...]))
-    take(1)
     take(7)
     need(0, 1)
 

time: 43.9 us -> 42.8 us (0.975)
  the two profiles are of different devices: /device:TPU:7 before, /device:TPU:1 now
where the time goes in v5:
time: 42.8 us; the launch traced here: 42.6 us
  Pallas kernels  41 us (96%)
  local copies, waits for them, and re-layouts  1.56 us (4%)
    pallas_call x1, Pallas kernels, shards(): pl.pallas_call(whole_kernel, out_shape=jax.ShapeDtypeStruct((48, 576), F3...  41 us
    unnamed x1, local copies, waits for them, and re-layouts  1.56 us

profile of v5, /device:TPU:1, one launch (start us, length us, event | category | flops | bytes accessed | tf_op | source)
XLA Modules:
  0.0 42.6 jit_solution(5479456735786481063)
XLA Ops:
  0.0 41.0 %shard_map.82 = f32[48,576]{1,0:T(8,128)} custom-call(s32[8]{0:T(128)} %partner_ref.1, s32[16,16]{1,0:T(8,128)} %index_ref.1, bf16[48,576]{1,0:T(8,128)(2,1)} %bitcast.5, f32[48,576]{1,0:T(8,128)} %bitcast.4, f32[16,24,576]{2,1,0:T(8,128)} %kernels_hbm.1, bf16[576,640]{1,0:T(8,128)(2,1)} %constant.6.clone.table_hbm, ...), custom_call_target="tpu_custom_call" | custom-call | tf_op jit(solution)/shard_map/pallas_call | solution.py:443
  41.0 1.6 %copy.10 = f32[1,2,24,576]{3,2,1,0:T(8,128)} copy(f32[1,2,24,576]{3,2,1,0:T(8,128)} %bitcast.3) | data formatting | bytes 221184

commit v6 on v5

--- a/solution.py
+++ b/solution.py
@@ -407,10 +407,9 @@
     steps = {
         (0, 0): lambda: take(2),
         (0, 1): lambda: take(3),
-        (0, 4): lambda: need(2, 3),
-        (1, 0): lambda: take(6),
-        (1, 1): lambda: take(5),
-        (1, 3): lambda: take(4),
+        (0, 4): lambda: (need(2, 3), take(6))[0],
+        (1, 0): lambda: take(5),
+        (1, 1): lambda: take(4),
         (1, 4): lambda: need(4, 5, 6, 7),
         (2, 4): give_back,
     }

time: 42.8 us -> 42.4 us (level)
    pallas_call x1, Pallas kernels: 41 us -> 40.6 us  [shards(): pl.pallas_call(whole_kernel, out_shape=jax.ShapeDtypeStruct((48, 576), F3...]
where the time goes in v6:
time: 42.4 us; the launch traced here: 42.1 us
  Pallas kernels  40.6 us (96%)
  local copies, waits for them, and re-layouts  1.56 us (4%)
    pallas_call x1, Pallas kernels, shards(): pl.pallas_call(whole_kernel, out_shape=jax.ShapeDtypeStruct((48, 576), F3...  40.6 us
    unnamed x1, local copies, waits for them, and re-layouts  1.56 us

profile of v6, /device:TPU:1, one launch (start us, length us, event | category | flops | bytes accessed | tf_op | source)
XLA Modules:
  0.0 42.1 jit_solution(12137037040595597613)
XLA Ops:
  0.0 40.6 %shard_map.82 = f32[48,576]{1,0:T(8,128)} custom-call(s32[8]{0:T(128)} %partner_ref.1, s32[16,16]{1,0:T(8,128)} %index_ref.1, bf16[48,576]{1,0:T(8,128)(2,1)} %bitcast.5, f32[48,576]{1,0:T(8,128)} %bitcast.4, f32[16,24,576]{2,1,0:T(8,128)} %kernels_hbm.1, bf16[576,640]{1,0:T(8,128)(2,1)} %constant.6.clone.table_hbm, ...), custom_call_target="tpu_custom_call" | custom-call | tf_op jit(solution)/shard_map/pallas_call | solution.py:442
  40.6 1.6 %copy.10 = f32[1,2,24,576]{3,2,1,0:T(8,128)} copy(f32[1,2,24,576]{3,2,1,0:T(8,128)} %bitcast.3) | data formatting | bytes 221184
